TPU v7x, 768 devices: a whole 4x8x12 slice. The times are simulated.
768 devices in a mesh: depth: 16 (over y_hi, x), height: 12 (over z), filt: 4 (over y_lo, core).
Axes of the slice: x: 4, y: 8 (y_hi: 4, y_lo: 2; y = y_hi * 2 + y_lo), z: 12, core: 2. Of those that a mesh axis runs over, the one named last changes fastest.
Arguments:
- volume: bfloat16 [64, 48, 64, 256], P('depth', 'height', None, 'filt'), may hold values from -6 to 6
- kernel_one: bfloat16 [3, 3, 3, 256, 256], replicated, may hold values from -0.078125 to 0.078125
- bias_one: float32 [256], replicated, may hold values from -3 to 3
- kernel_two: bfloat16 [3, 3, 3, 256, 256], replicated, may hold values from -0.078125 to 0.078125
- bias_two: float32 [256], replicated, may hold values from -3 to 3
Outputs:
- features: bfloat16 [64, 48, 64, 256], P('depth', 'height', None, 'filt')
All inputs are finite; a program needn't handle non-finite values.
Results may differ from a plain program's by a relative error of at most 0.0044.
Values may be sent and summed in bfloat16 or wider, within the bound.
A program may use at most 32 MiB of HBM per device.

v0:
```python
import jax
import jax.numpy as jnp
from jax import lax
from jax.sharding import PartitionSpec as P


def extended(x, sides, width):
    for axis, dim in sides:
        peers, length = (lax.axis_size(axis), x.shape[dim])
        up = [(i, (i + 1) % peers) for i in range(peers - 1)]
        down = [(j, i) for i, j in up]
        last = lax.slice_in_dim(x, length - width, length, axis=dim)
        initial = lax.slice_in_dim(x, 0, width, axis=dim)
        before = lax.ppermute(last, axis, up)
        after = lax.ppermute(initial, axis, down)
        x = jnp.concatenate([before, x, after], axis=dim)
    return x


def leaky(value):
    return jnp.where(value > 0, value, 0.3 * value)


def convolve(padded, kernel, width_pad):
    out = lax.conv_general_dilated(
        padded[None],
        kernel,
        (1, 1, 1),
        [(0, 0), (0, 0), (width_pad, width_pad)],
        dimension_numbers=("NDHWC", "DHWIO", "NDHWC"),
        preferred_element_type=jnp.float32,
    )
    return out[0]


def body(volume, kernel_one, bias_one, kernel_two, bias_two):
    shard = volume.shape[3]
    offset = lax.axis_index("filt") * shard
    whole = lax.all_gather(volume, "filt", axis=3, tiled=True)
    padded = extended(whole, (("depth", 0), ("height", 1)), 1)
    kernel_own = lax.dynamic_slice_in_dim(kernel_one, offset, shard, 4)
    bias_own = lax.dynamic_slice_in_dim(bias_one, offset, shard, 0)
    hidden = leaky(convolve(padded, kernel_own, 1) + bias_own).astype(jnp.bfloat16)
    bias_last = lax.dynamic_slice_in_dim(bias_two, offset, shard, 0)
    hidden_whole = lax.all_gather(hidden, "filt", axis=3, tiled=True)
    hidden_padded = extended(hidden_whole, (("depth", 0), ("height", 1)), 1)
    kernel_last = lax.dynamic_slice_in_dim(kernel_two, offset, shard, 4)
    summed = convolve(hidden_padded, kernel_last, 1)
    return leaky(summed + bias_last).astype(jnp.bfloat16)


def solution(mesh):
    in_specs = (P("depth", "height", None, "filt"), P(), P(), P(), P())
    out_specs = P("depth", "height", None, "filt")
    return jax.shard_map(body, mesh=mesh, in_specs=in_specs, out_specs=out_specs, check_vma=False)
```

profile of v0, /device:TPU:86, one launch (start us, length us, event | category | flops | bytes accessed | tf_op | source)
XLA Modules:
  0.0 133.8 jit_solution(10036521288510648378)
XLA Ops:
  0.0 0.0 copy-start
  0.0 2.0 %copy.31 = bf16[4,4,64,64]{2,1,0,3:T(4,128)(2,1)} copy(bf16[4,4,64,64]{3,2,1,0:T(8,128)(2,1)} %param.5) | data formatting | bytes 262144 | tf_op args[0]
  2.0 10.3 %all_gather.6 = bf16[4,4,64,256]{2,1,0,3:T(4,128)(2,1)S(1)} all-gather(bf16[4,4,64,64]{2,1,0,3:T(4,128)(2,1)} %copy.31), channel_id=1, replica_groups=mesh['depth'=16,'height'=12,'filt'=4] {'filt'}, dimensions={3}, use_global_device_ids=true | all-gather | bytes 655360 | tf_op jit(solution)/shard_map/all_gather | solution.py:39
  12.3 0.2 fusion.45
  12.5 5.1 %collective-permute-start = (bf16[1,4,64,256]{2,1,0,3:T(4,128)(2,1)S(1)}, bf16[1,4,64,256]{2,1,0,3:T(4,128)(2,1)S(1)}, u32[]{:S(2)}, u32[]{:S(2)}) collective-permute-start(bf16[1,4,64,256]{2,1,0,3:T(4,128)(2,1)S(1)} %get-tuple-element.12), channel_id=1, source_target_pairs={{0,48},{48,96},{96,144},{144,192},{192,240},{240,288},{288,336},{3... | collective-permute-start | bytes 393224 | tf_op jit(solution)/shard_map/ppermute | solution.py:14
  17.7 1.9 %collective-permute-start.1 = (bf16[1,4,64,256]{2,1,0,3:T(4,128)(2,1)S(1)}, bf16[1,4,64,256]{2,1,0,3:T(4,128)(2,1)S(1)}, u32[]{:S(2)}, u32[]{:S(2)}) collective-permute-start(bf16[1,4,64,256]{2,1,0,3:T(4,128)(2,1)S(1)} %get-tuple-element.11), channel_id=1, source_target_pairs={{48,0},{96,48},{144,96},{192,144},{240,192},{288,240},{336,288},{3... | collective-permute-start | bytes 393224 | tf_op jit(solution)/shard_map/ppermute | solution.py:15
  19.6 9.3 %collective-permute-done = bf16[1,4,64,256]{2,1,0,3:T(4,128)(2,1)S(1)} collective-permute-done((bf16[1,4,64,256]{2,1,0,3:T(4,128)(2,1)S(1)}, bf16[1,4,64,256]{2,1,0,3:T(4,128)(2,1)S(1)}, u32[]{:S(2)}, u32[]{:S(2)}) %collective-permute-start) | collective-permute-done | bytes 131104 | tf_op jit(solution)/shard_map/ppermute | solution.py:14
  28.9 0.1 constant_dynamic-update-slice_fusion.2
  29.0 0.5 constant_dynamic-update-slice_fusion.1
  29.5 7.4 %collective-permute-done.1 = bf16[1,4,64,256]{2,1,0,3:T(4,128)(2,1)S(1)} collective-permute-done((bf16[1,4,64,256]{2,1,0,3:T(4,128)(2,1)S(1)}, bf16[1,4,64,256]{2,1,0,3:T(4,128)(2,1)S(1)}, u32[]{:S(2)}, u32[]{:S(2)}) %collective-permute-start.1) | collective-permute-done | bytes 131104 | tf_op jit(solution)/shard_map/ppermute | solution.py:15
  36.9 0.2 constant_dynamic-update-slice_fusion
  37.0 0.0 copy-start.1
  37.1 2.2 %fusion.43 = (bf16[6,1,64,256]{2,1,0,3:T(2,128)(2,1)}, bf16[6,1,64,256]{2,1,0,3:T(2,128)(2,1)}) fusion(bf16[6,4,64,256]{2,1,0,3:T(4,128)(2,1)S(1)} %constant_dynamic-update-slice_fusion), kind=kLoop, calls=%fused_computation.46 | loop fusion | bytes 786432 | tf_op jit(solution)/shard_map/slice | solution.py:12
  39.3 2.8 %copy.32 = bf16[6,1,64,256]{3,2,1,0:T(8,128)(2,1)} copy(bf16[6,1,64,256]{2,1,0,3:T(2,128)(2,1)} %get-tuple-element.7) | data formatting | bytes 393216 | tf_op jit(solution)/shard_map/slice | solution.py:12
  42.1 4.3 %collective-permute-start.2 = (bf16[6,1,64,256]{3,2,1,0:T(8,128)(2,1)}, bf16[6,1,64,256]{3,2,1,0:T(8,128)(2,1)}, u32[]{:S(2)}, u32[]{:S(2)}) collective-permute-start(bf16[6,1,64,256]{3,2,1,0:T(8,128)(2,1)} %copy.32), channel_id=1, source_target_pairs={{0,4},{4,8},{8,12},{12,16},{16,20},{20,24},{24,28},{28,32},{32,36}... | collective-permute-start | bytes 589832 | tf_op jit(solution)/shard_map/ppermute | solution.py:14
  46.3 2.8 %copy.33 = bf16[6,1,64,256]{3,2,1,0:T(8,128)(2,1)} copy(bf16[6,1,64,256]{2,1,0,3:T(2,128)(2,1)} %get-tuple-element.8) | data formatting | bytes 393216 | tf_op jit(solution)/shard_map/slice | solution.py:13
  49.1 2.2 %collective-permute-start.3 = (bf16[6,1,64,256]{3,2,1,0:T(8,128)(2,1)}, bf16[6,1,64,256]{3,2,1,0:T(8,128)(2,1)}, u32[]{:S(2)}, u32[]{:S(2)}) collective-permute-start(bf16[6,1,64,256]{3,2,1,0:T(8,128)(2,1)} %copy.33), channel_id=1, source_target_pairs={{4,0},{8,4},{12,8},{16,12},{20,16},{24,20},{28,24},{32,28},{36,32}... | collective-permute-start | bytes 589832 | tf_op jit(solution)/shard_map/ppermute | solution.py:15
  51.4 0.0 copy-done.4
  51.4 0.1 dynamic_slice.13
  51.5 3.5 %copy.34 = bf16[6,4,64,256]{3,2,1,0:T(8,128)(2,1)} copy(bf16[6,4,64,256]{2,1,0,3:T(4,128)(2,1)} %copy-done.1) | data formatting | bytes 1572864 | tf_op jit(solution)/shard_map/concatenate | solution.py:16
  54.9 0.0 collective-permute-done.2
  54.9 3.2 %collective-permute-done.3 = bf16[6,1,64,256]{3,2,1,0:T(8,128)(2,1)} collective-permute-done((bf16[6,1,64,256]{3,2,1,0:T(8,128)(2,1)}, bf16[6,1,64,256]{3,2,1,0:T(8,128)(2,1)}, u32[]{:S(2)}, u32[]{:S(2)}) %collective-permute-start.3) | collective-permute-done | bytes 196640 | tf_op jit(solution)/shard_map/ppermute | solution.py:15
  58.1 1.4 %maximum_bitcast_fusion = bf16[6,6,1,64,256]{4,3,1,0,2:T(8,128)(2,1)S(1)} fusion(bf16[6,1,64,256]{3,2,1,0:T(8,128)(2,1)} %collective-permute-done.3, bf16[6,4,64,256]{3,2,1,0:T(8,128)(2,1)} %copy.34, bf16[6,1,64,256]{3,2,1,0:T(8,128)(2,1)} %collective-permute-done.2), kind=kLoop, calls=%fused_computation.21 | loop fusion | flops 1179648 | bytes 2359296 | tf_op jit(solution)/shard_map/broadcast_in_dim | solution.py:26
  59.5 0.8 copy.52
  60.3 0.3 pad.clone
  60.6 0.0 copy-start.6
  60.6 0.3 copy.37
  60.9 0.1 slice.40
  61.0 0.0 copy-done
  61.0 0.3 copy-done.6
  61.3 4.4 %fusion.18 = f32[4,4,8,9,64]{4,2,3,1,0:T(8,128)S(1)} fusion(bf16[3,3,3,256,256]{4,3,2,1,0:T(8,128)(2,1)S(1)} %copy-done, s32[]{:T(128)S(6)} %select_n.13, bf16[6,6,1,7,2,256]{5,3,4,1,0,2:T(8,128)(2,1)S(1)} %slice.40, bf16[6,6,1,8,9,256]{5,3,4,1,0,2:T(8,128)(2,1)S(1)} %copy.37, pred[8,9]{0,1:T(8,128)(4,1)S(1)} %copy-done.6), kind=kOutput, calls=%fused_computation.19 | convolution fusion | flops 1024155648 | bytes 3688452 | tf_op jit(solution)/shard_map/conv_general_dilated | solution.py:25
  65.8 0.2 copy.39
  65.9 0.9 fusion.30
  66.8 1.9 %copy.40 = bf16[4,4,64,64]{2,1,0,3:T(4,128)(2,1)} copy(bf16[4,4,64,64]{3,1,2,0:T(4,128)(2,1)} %fusion.30) | data formatting | bytes 262144 | tf_op jit(solution)/shard_map/convert_element_type | solution.py:43
  68.7 9.3 %all_gather.7 = bf16[4,4,64,256]{2,1,0,3:T(4,128)(2,1)S(1)} all-gather(bf16[4,4,64,64]{2,1,0,3:T(4,128)(2,1)} %copy.40), channel_id=1, replica_groups=mesh['depth'=16,'height'=12,'filt'=4] {'filt'}, dimensions={3}, use_global_device_ids=true | all-gather | bytes 655360 | tf_op jit(solution)/shard_map/all_gather | solution.py:45
  78.1 0.2 fusion.44
  78.3 1.9 %collective-permute-start.4 = (bf16[1,4,64,256]{2,1,0,3:T(4,128)(2,1)S(1)}, bf16[1,4,64,256]{2,1,0,3:T(4,128)(2,1)S(1)}, u32[]{:S(2)}, u32[]{:S(2)}) collective-permute-start(bf16[1,4,64,256]{2,1,0,3:T(4,128)(2,1)S(1)} %get-tuple-element.10), channel_id=1, source_target_pairs={{0,48},{48,96},{96,144},{144,192},{192,240},{240,288},{288,336},{3... | collective-permute-start | bytes 393224 | tf_op jit(solution)/shard_map/ppermute | solution.py:14
  80.2 4.1 %collective-permute-start.5 = (bf16[1,4,64,256]{2,1,0,3:T(4,128)(2,1)S(1)}, bf16[1,4,64,256]{2,1,0,3:T(4,128)(2,1)S(1)}, u32[]{:S(2)}, u32[]{:S(2)}) collective-permute-start(bf16[1,4,64,256]{2,1,0,3:T(4,128)(2,1)S(1)} %get-tuple-element.9), channel_id=1, source_target_pairs={{48,0},{96,48},{144,96},{192,144},{240,192},{288,240},{336,288},{3... | collective-permute-start | bytes 393224 | tf_op jit(solution)/shard_map/ppermute | solution.py:15
  84.3 7.8 %collective-permute-done.4 = bf16[1,4,64,256]{2,1,0,3:T(4,128)(2,1)S(1)} collective-permute-done((bf16[1,4,64,256]{2,1,0,3:T(4,128)(2,1)S(1)}, bf16[1,4,64,256]{2,1,0,3:T(4,128)(2,1)S(1)}, u32[]{:S(2)}, u32[]{:S(2)}) %collective-permute-start.4) | collective-permute-done | bytes 131104 | tf_op jit(solution)/shard_map/ppermute | solution.py:14
  92.1 0.1 constant_dynamic-update-slice_fusion.5
  92.2 0.5 constant_dynamic-update-slice_fusion.4
  92.6 7.8 %collective-permute-done.5 = bf16[1,4,64,256]{2,1,0,3:T(4,128)(2,1)S(1)} collective-permute-done((bf16[1,4,64,256]{2,1,0,3:T(4,128)(2,1)S(1)}, bf16[1,4,64,256]{2,1,0,3:T(4,128)(2,1)S(1)}, u32[]{:S(2)}, u32[]{:S(2)}) %collective-permute-start.5) | collective-permute-done | bytes 131104 | tf_op jit(solution)/shard_map/ppermute | solution.py:15
  100.5 0.2 constant_dynamic-update-slice_fusion.3
  100.7 2.2 %fusion.42 = (bf16[6,1,64,256]{2,1,0,3:T(2,128)(2,1)}, bf16[6,1,64,256]{2,1,0,3:T(2,128)(2,1)}) fusion(bf16[6,4,64,256]{2,1,0,3:T(4,128)(2,1)S(1)} %constant_dynamic-update-slice_fusion.3), kind=kLoop, calls=%fused_computation.45 | loop fusion | bytes 786432 | tf_op jit(solution)/shard_map/slice | solution.py:12
  102.9 0.0 copy-done.2
  102.9 2.8 %copy.41 = bf16[6,1,64,256]{3,2,1,0:T(8,128)(2,1)} copy(bf16[6,1,64,256]{2,1,0,3:T(2,128)(2,1)} %get-tuple-element.5) | data formatting | bytes 393216 | tf_op jit(solution)/shard_map/slice | solution.py:12
  105.7 5.5 %collective-permute-start.6 = (bf16[6,1,64,256]{3,2,1,0:T(8,128)(2,1)}, bf16[6,1,64,256]{3,2,1,0:T(8,128)(2,1)}, u32[]{:S(2)}, u32[]{:S(2)}) collective-permute-start(bf16[6,1,64,256]{3,2,1,0:T(8,128)(2,1)} %copy.41), channel_id=1, source_target_pairs={{0,4},{4,8},{8,12},{12,16},{16,20},{20,24},{24,28},{28,32},{32,36}... | collective-permute-start | bytes 589832 | tf_op jit(solution)/shard_map/ppermute | solution.py:14
  111.2 2.8 %copy.42 = bf16[6,1,64,256]{3,2,1,0:T(8,128)(2,1)} copy(bf16[6,1,64,256]{2,1,0,3:T(2,128)(2,1)} %get-tuple-element.6) | data formatting | bytes 393216 | tf_op jit(solution)/shard_map/slice | solution.py:13
  114.0 1.9 %collective-permute-start.7 = (bf16[6,1,64,256]{3,2,1,0:T(8,128)(2,1)}, bf16[6,1,64,256]{3,2,1,0:T(8,128)(2,1)}, u32[]{:S(2)}, u32[]{:S(2)}) collective-permute-start(bf16[6,1,64,256]{3,2,1,0:T(8,128)(2,1)} %copy.42), channel_id=1, source_target_pairs={{4,0},{8,4},{12,8},{16,12},{20,16},{24,20},{28,24},{32,28},{36,32}... | collective-permute-start | bytes 589832 | tf_op jit(solution)/shard_map/ppermute | solution.py:15
  115.9 0.1 dynamic_slice.15
  116.0 3.5 %copy.43 = bf16[6,4,64,256]{3,2,1,0:T(8,128)(2,1)} copy(bf16[6,4,64,256]{2,1,0,3:T(4,128)(2,1)} %copy-done.2) | data formatting | bytes 1572864 | tf_op jit(solution)/shard_map/concatenate | solution.py:16
  119.4 0.0 collective-permute-done.6
  119.4 4.3 %collective-permute-done.7 = bf16[6,1,64,256]{3,2,1,0:T(8,128)(2,1)} collective-permute-done((bf16[6,1,64,256]{3,2,1,0:T(8,128)(2,1)}, bf16[6,1,64,256]{3,2,1,0:T(8,128)(2,1)}, u32[]{:S(2)}, u32[]{:S(2)}) %collective-permute-start.7) | collective-permute-done | bytes 196640 | tf_op jit(solution)/shard_map/ppermute | solution.py:15
  123.7 1.4 %maximum_bitcast_fusion.1 = bf16[6,6,1,64,256]{4,3,1,0,2:T(8,128)(2,1)S(1)} fusion(bf16[6,1,64,256]{3,2,1,0:T(8,128)(2,1)} %collective-permute-done.7, bf16[6,4,64,256]{3,2,1,0:T(8,128)(2,1)} %copy.43, bf16[6,1,64,256]{3,2,1,0:T(8,128)(2,1)} %collective-permute-done.6), kind=kLoop, calls=%fused_computation.22 | loop fusion | flops 1179648 | bytes 2359296 | tf_op jit(solution)/shard_map/broadcast_in_dim | solution.py:26
  125.1 0.8 copy.53
  125.8 0.3 pad.2.clone
  126.2 0.0 copy-start.3
  126.2 0.3 copy.46
  126.5 0.1 slice.46
  126.6 1.6 %copy-done.3 = bf16[3,3,3,256,256]{4,3,2,1,0:T(8,128)(2,1)S(1)} copy-done((bf16[3,3,3,256,256]{4,3,2,1,0:T(8,128)(2,1)S(1)}, bf16[3,3,3,256,256]{4,3,2,1,0:T(8,128)(2,1)}, u32[]{:S(2)}) %copy-start.3) | copy-done | bytes 3538968
  128.2 4.5 %fusion.23 = f32[4,4,8,9,64]{4,2,3,1,0:T(8,128)S(1)} fusion(bf16[3,3,3,256,256]{4,3,2,1,0:T(8,128)(2,1)S(1)} %copy-done.3, s32[]{:T(128)S(6)} %select_n.13, bf16[6,6,1,7,2,256]{5,3,4,1,0,2:T(8,128)(2,1)S(1)} %slice.46, bf16[6,6,1,8,9,256]{5,3,4,1,0,2:T(8,128)(2,1)S(1)} %copy.46, pred[8,9]{0,1:T(8,128)(4,1)S(1)} %copy-done.6), kind=kOutput, calls=%fused_computation.20 | convolution fusion | flops 1024155648 | bytes 3688452 | tf_op jit(solution)/shard_map/conv_general_dilated | solution.py:25
  132.7 0.2 copy.48
  132.8 0.2 fusion.31
  133.0 0.8 copy.49
  (5 shorter events, 0.0 us)
Async XLA Ops:
  0.0 61.0 %copy-start = (bf16[3,3,3,256,256]{4,3,2,1,0:T(8,128)(2,1)S(1)}, bf16[3,3,3,256,256]{4,3,2,1,0:T(8,128)(2,1)}, u32[]{:S(2)}) copy-start(bf16[3,3,3,256,256]{4,3,2,1,0:T(8,128)(2,1)} %param.6) | copy-start | bytes 10616836
  12.5 16.4 %collective-permute-start = (bf16[1,4,64,256]{2,1,0,3:T(4,128)(2,1)S(1)}, bf16[1,4,64,256]{2,1,0,3:T(4,128)(2,1)S(1)}, u32[]{:S(2)}, u32[]{:S(2)}) collective-permute-start(bf16[1,4,64,256]{2,1,0,3:T(4,128)(2,1)S(1)} %get-tuple-element.12), channel_id=1, source_target_pairs={{0,48},{48,96},{96,144},{144,192},{192,240},{240,288},{288,336},{3... | collective-permute-start | bytes 393224 | tf_op jit(solution)/shard_map/ppermute | solution.py:14
  17.7 19.2 %collective-permute-start.1 = (bf16[1,4,64,256]{2,1,0,3:T(4,128)(2,1)S(1)}, bf16[1,4,64,256]{2,1,0,3:T(4,128)(2,1)S(1)}, u32[]{:S(2)}, u32[]{:S(2)}) collective-permute-start(bf16[1,4,64,256]{2,1,0,3:T(4,128)(2,1)S(1)} %get-tuple-element.11), channel_id=1, source_target_pairs={{48,0},{96,48},{144,96},{192,144},{240,192},{288,240},{336,288},{3... | collective-permute-start | bytes 393224 | tf_op jit(solution)/shard_map/ppermute | solution.py:15
  37.0 2.2 %copy-start.1 = (bf16[6,4,64,256]{2,1,0,3:T(4,128)(2,1)}, bf16[6,4,64,256]{2,1,0,3:T(4,128)(2,1)S(1)}, u32[]{:S(2)}) copy-start(bf16[6,4,64,256]{2,1,0,3:T(4,128)(2,1)S(1)} %constant_dynamic-update-slice_fusion) | copy-start | bytes 2359300
  39.3 12.1 %copy-start.4 = (f32[256]{0:T(256)S(1)}, f32[256]{0:T(256)}, u32[]{:S(2)}) copy-start(f32[256]{0:T(256)} %param.7) | copy-start | bytes 3076
  42.1 12.9 %collective-permute-start.2 = (bf16[6,1,64,256]{3,2,1,0:T(8,128)(2,1)}, bf16[6,1,64,256]{3,2,1,0:T(8,128)(2,1)}, u32[]{:S(2)}, u32[]{:S(2)}) collective-permute-start(bf16[6,1,64,256]{3,2,1,0:T(8,128)(2,1)} %copy.32), channel_id=1, source_target_pairs={{0,4},{4,8},{8,12},{12,16},{16,20},{20,24},{24,28},{28,32},{32,36}... | collective-permute-start | bytes 589832 | tf_op jit(solution)/shard_map/ppermute | solution.py:14
  49.1 9.0 %collective-permute-start.3 = (bf16[6,1,64,256]{3,2,1,0:T(8,128)(2,1)}, bf16[6,1,64,256]{3,2,1,0:T(8,128)(2,1)}, u32[]{:S(2)}, u32[]{:S(2)}) collective-permute-start(bf16[6,1,64,256]{3,2,1,0:T(8,128)(2,1)} %copy.33), channel_id=1, source_target_pairs={{4,0},{8,4},{12,8},{16,12},{20,16},{24,20},{28,24},{32,28},{36,32}... | collective-permute-start | bytes 589832 | tf_op jit(solution)/shard_map/ppermute | solution.py:15
  60.6 0.7 copy-start.6
  78.3 13.8 %collective-permute-start.4 = (bf16[1,4,64,256]{2,1,0,3:T(4,128)(2,1)S(1)}, bf16[1,4,64,256]{2,1,0,3:T(4,128)(2,1)S(1)}, u32[]{:S(2)}, u32[]{:S(2)}) collective-permute-start(bf16[1,4,64,256]{2,1,0,3:T(4,128)(2,1)S(1)} %get-tuple-element.10), channel_id=1, source_target_pairs={{0,48},{48,96},{96,144},{144,192},{192,240},{240,288},{288,336},{3... | collective-permute-start | bytes 393224 | tf_op jit(solution)/shard_map/ppermute | solution.py:14
  80.2 20.3 %collective-permute-start.5 = (bf16[1,4,64,256]{2,1,0,3:T(4,128)(2,1)S(1)}, bf16[1,4,64,256]{2,1,0,3:T(4,128)(2,1)S(1)}, u32[]{:S(2)}, u32[]{:S(2)}) collective-permute-start(bf16[1,4,64,256]{2,1,0,3:T(4,128)(2,1)S(1)} %get-tuple-element.9), channel_id=1, source_target_pairs={{48,0},{96,48},{144,96},{192,144},{240,192},{288,240},{336,288},{3... | collective-permute-start | bytes 393224 | tf_op jit(solution)/shard_map/ppermute | solution.py:15
  100.7 2.2 %copy-start.2 = (bf16[6,4,64,256]{2,1,0,3:T(4,128)(2,1)}, bf16[6,4,64,256]{2,1,0,3:T(4,128)(2,1)S(1)}, u32[]{:S(2)}) copy-start(bf16[6,4,64,256]{2,1,0,3:T(4,128)(2,1)S(1)} %constant_dynamic-update-slice_fusion.3) | copy-start | bytes 2359300
  102.9 13.0 %copy-start.5 = (f32[256]{0:T(256)S(1)}, f32[256]{0:T(256)}, u32[]{:S(2)}) copy-start(f32[256]{0:T(256)} %param.9) | copy-start | bytes 3076
  105.7 13.7 %collective-permute-start.6 = (bf16[6,1,64,256]{3,2,1,0:T(8,128)(2,1)}, bf16[6,1,64,256]{3,2,1,0:T(8,128)(2,1)}, u32[]{:S(2)}, u32[]{:S(2)}) collective-permute-start(bf16[6,1,64,256]{3,2,1,0:T(8,128)(2,1)} %copy.41), channel_id=1, source_target_pairs={{0,4},{4,8},{8,12},{12,16},{16,20},{20,24},{24,28},{28,32},{32,36}... | collective-permute-start | bytes 589832 | tf_op jit(solution)/shard_map/ppermute | solution.py:14
  114.0 9.7 %collective-permute-start.7 = (bf16[6,1,64,256]{3,2,1,0:T(8,128)(2,1)}, bf16[6,1,64,256]{3,2,1,0:T(8,128)(2,1)}, u32[]{:S(2)}, u32[]{:S(2)}) collective-permute-start(bf16[6,1,64,256]{3,2,1,0:T(8,128)(2,1)} %copy.42), channel_id=1, source_target_pairs={{4,0},{8,4},{12,8},{16,12},{20,16},{24,20},{28,24},{32,28},{36,32}... | collective-permute-start | bytes 589832 | tf_op jit(solution)/shard_map/ppermute | solution.py:15
  126.2 2.0 %copy-start.3 = (bf16[3,3,3,256,256]{4,3,2,1,0:T(8,128)(2,1)S(1)}, bf16[3,3,3,256,256]{4,3,2,1,0:T(8,128)(2,1)}, u32[]{:S(2)}) copy-start(bf16[3,3,3,256,256]{4,3,2,1,0:T(8,128)(2,1)} %param.8) | copy-start | bytes 10616836
where the time goes:
time: 134 us
  waiting for transfers between devices  39.8 us (30%)
  local copies, waits for them, and re-layouts  34.3 us (26%)
  starting transfers between devices  27 us (20%)
  blocking collectives  19.6 us (15%)
  matrix products  8.9 us (7%)
  other arithmetic  3.86 us (3%)
    ppermute x4, waiting for transfers between devices, extended(): after = lax.ppermute(initial, axis, down)  22.7 us
    ppermute x4, waiting for transfers between devices, extended(): before = lax.ppermute(last, axis, up)  17.1 us
    ppermute x4, starting transfers between devices, extended(): before = lax.ppermute(last, axis, up)  16.8 us
    all_gather x1, blocking collectives, body(): whole = lax.all_gather(volume, 'filt', axis=3, tiled=True)  10.3 us
    ppermute x4, starting transfers between devices, extended(): after = lax.ppermute(initial, axis, down)  10.2 us
    slice x4, local copies, waits for them, and re-layouts, extended(): last = lax.slice_in_dim(x, length - width, length, axis=dim)  10 us
    all_gather x1, blocking collectives, body(): hidden_whole = lax.all_gather(hidden, 'filt', axis=3, tiled=True)  9.34 us
    conv_general_dilated x2, matrix products, convolve(): lax.conv_general_dilated(padded[None], kernel, (1, 1, 1), [(0, 0), (0, 0)...  8.9 us
  transfers between devices with their start and end apart: 8, of which 6 were waited for; matrix products, arithmetic and copies ran while one was open for 10% of the time, Pallas kernels for 0%

commit v1 on v0

v1 whole, which is shorter than its diff:
```python
import functools

import jax
import jax.numpy as jnp
from jax import lax
from jax.experimental import pallas as pl
from jax.experimental.pallas import tpu as pltpu
from jax.sharding import PartitionSpec as P

MESH = pl.DeviceIdType.MESH
DIRS = ((-1, 0), (1, 0), (0, -1), (0, 1), (-1, -1), (-1, 1), (1, -1), (1, 1))


def opposite(k):
    return DIRS.index((-DIRS[k][0], -DIRS[k][1]))


def halo_part(step):
    return pl.ds({-1: 0, 0: 1, 1: 3}[step], 2 if step == 0 else 1)


def edge_part(step):
    return pl.ds({-1: 1, 0: 1, 1: 2}[step], 2 if step == 0 else 1)


def flip_of(d):
    return (d % 2) * (1 - (d % 4) // 2)


def leaky(value):
    return jnp.where(value > 0, value, 0.3 * value)


def convolve(x, w, bias):
    width, chans = x.shape[2], x.shape[3]
    rows = 4 * width
    sums = []
    for c in range(3):
        acc = None
        for a in range(3):
            for b in range(3):
                lhs = x[a : a + 2, b : b + 2].reshape(rows, chans)
                part = jnp.dot(lhs, w[a, b, c], preferred_element_type=jnp.float32)
                acc = part if acc is None else acc + part
        sums.append(acc)
    w_of = lax.rem(lax.broadcasted_iota(jnp.int32, (rows, chans), 0), width)
    low = jnp.where(w_of == 0, 0.0, pltpu.roll(sums[0], 1, 0))
    high = jnp.where(w_of == width - 1, 0.0, pltpu.roll(sums[2], rows - 1, 0))
    total = low + sums[1] + high + bias[...]
    return leaky(total).astype(jnp.bfloat16)


def kernel(
    depths, heights,
    vol, k1, b1, k2, b2, out,
    xv, w1, w2, bb1, bb2, xs, ra, xh, hh, os,
    lsem, sa, qa, sb, qb, sc, qc, se, qe,
):
    d, h, f = lax.axis_index("depth"), lax.axis_index("height"), lax.axis_index("filt")
    flip = flip_of(d)
    fd, fh = (f // 2 + flip) % 2, f % 2
    quarter = 2 * fd + fh
    fine_d, fine_h = 2 * d + fd, 2 * h + fh
    width, shard = vol.shape[2], vol.shape[3]
    rows = 3 - jnp.where(fine_d == 0, 1, 0) - jnp.where(fine_d == 2 * depths - 1, 1, 0)
    columns = 3 - jnp.where(fine_h == 0, 1, 0) - jnp.where(fine_h == 2 * heights - 1, 1, 0)
    peers = rows * columns - 1

    def neighbour(k):
        nd, nh = fine_d + DIRS[k][0], fine_h + DIRS[k][1]
        block = nd // 2
        nf = 2 * ((nd + flip_of(block)) % 2) + nh % 2
        valid = (nd >= 0) & (nd < 2 * depths) & (nh >= 0) & (nh < 2 * heights)
        return valid, {"depth": block, "height": nh // 2, "filt": nf}

    loads = [
        pltpu.make_async_copy(src, dst, lsem.at[i])
        for i, (src, dst) in enumerate(((vol, xv), (b1, bb1), (b2, bb2), (k1, w1), (k2, w2)))
    ]
    for load in loads:
        load.start()

    barrier = pltpu.get_barrier_semaphore()
    for k in range(8):
        valid, device = neighbour(k)

        @pl.when(valid)
        def _():
            pl.semaphore_signal(barrier, inc=1, device_id=device, device_id_type=MESH)

    for k in range(8):
        valid, _ = neighbour(k)

        @pl.when(jnp.logical_not(valid))
        def _():
            part = (halo_part(DIRS[k][0]), halo_part(DIRS[k][1]))
            for ref in (xh, hh):
                ref[part] = jnp.zeros_like(ref[part])

    loads[0].wait()
    for q in range(4):
        top, side = 2 * (q // 2), 2 * (q % 2)
        xs[q] = jnp.concatenate([xv[top : top + 2, side], xv[top : top + 2, side + 1]], axis=-1)

    pl.semaphore_wait(barrier, peers)

    def gather(q):
        return pltpu.make_async_remote_copy(
            src_ref=xs.at[q], dst_ref=ra.at[f], send_sem=sa.at[q], recv_sem=qa.at[f],
            device_id={"filt": 2 * ((q // 2 + flip) % 2) + q % 2}, device_id_type=MESH)

    for q in range(4):
        @pl.when(q != quarter)
        def _():
            gather(q).start()

    ra[f] = xs[quarter]
    for g in range(4):
        @pl.when(g != f)
        def _():
            pltpu.make_async_remote_copy(
                src_ref=xs.at[0], dst_ref=ra.at[g], send_sem=sa.at[0], recv_sem=qa.at[g],
                device_id={"filt": g}, device_id_type=MESH).wait_recv()

    for i in range(2):
        for j in range(2):
            xh[1 + i, 1 + j] = jnp.concatenate(
                [ra[g, i, :, j * shard : (j + 1) * shard] for g in range(4)], axis=-1)

    def halo(ref, send, recv, k):
        valid, device = neighbour(k)
        sd, sh = DIRS[k]
        edge = ref.at[edge_part(sd), edge_part(sh)]

        def copy():
            return pltpu.make_async_remote_copy(
                src_ref=edge, dst_ref=ref.at[halo_part(-sd), halo_part(-sh)],
                send_sem=send.at[k], recv_sem=recv.at[opposite(k)],
                device_id=device, device_id_type=MESH)

        def arrival():
            return pltpu.make_async_remote_copy(
                src_ref=edge, dst_ref=ref.at[halo_part(sd), halo_part(sh)],
                send_sem=send.at[k], recv_sem=recv.at[k],
                device_id=device, device_id_type=MESH)

        return valid, copy, arrival

    def exchange(ref, send, recv):
        for k in reversed(range(8)):
            valid, copy, _ = halo(ref, send, recv, k)

            @pl.when(valid)
            def _():
                copy().start()

        for k in range(8):
            valid, _, arrival = halo(ref, send, recv, k)

            @pl.when(valid)
            def _():
                arrival().wait_recv()

    exchange(xh, sb, qb)
    loads[1].wait()
    loads[3].wait()
    hidden = convolve(xh, w1, bb1)
    hh[1:3, 1:3] = hidden.reshape(2, 2, width, 4 * shard)

    exchange(hh, sc, qc)
    loads[2].wait()
    loads[4].wait()
    result = convolve(hh, w2, bb2).reshape(2, 2, width, 4 * shard)
    for g in range(4):
        part = result[:, :, :, g * shard : (g + 1) * shard]
        os[g] = jnp.concatenate([part[:, 0], part[:, 1]], axis=-1)

    def scatter(g):
        return pltpu.make_async_remote_copy(
            src_ref=os.at[g], dst_ref=out.at[quarter], send_sem=se.at[g], recv_sem=qe.at[quarter],
            device_id={"filt": g}, device_id_type=MESH)

    for g in range(4):
        @pl.when(g != f)
        def _():
            scatter(g).start()

    own = pltpu.make_async_copy(os.at[f], out.at[quarter], lsem.at[5])
    own.start()
    own.wait()
    for q in range(4):
        @pl.when(q != quarter)
        def _():
            pltpu.make_async_remote_copy(
                src_ref=os.at[0], dst_ref=out.at[q], send_sem=se.at[0], recv_sem=qe.at[q],
                device_id={"filt": 2 * ((q // 2 + flip) % 2) + q % 2}, device_id_type=MESH).wait_recv()

    for q in range(4):
        @pl.when(q != quarter)
        def _():
            gather(q).wait_send()

        @pl.when(q != f)
        def _():
            scatter(q).wait_send()

    for k in range(8):
        valid, first, _ = halo(xh, sb, qb, k)
        _, second, _ = halo(hh, sc, qc, k)

        @pl.when(valid)
        def _():
            first().wait_send()
            second().wait_send()


def body(depths, heights, volume, kernel_one, bias_one, kernel_two, bias_two):
    _, _, width, shard = volume.shape
    chans = 4 * shard
    bf16, dma = jnp.bfloat16, pltpu.SemaphoreType.DMA
    packed = pltpu.VMEM((4, 2, width, 2 * shard), bf16)
    parts = pl.pallas_call(
        functools.partial(kernel, depths, heights),
        out_shape=jax.ShapeDtypeStruct((4, 2, width, 2 * shard), bf16),
        in_specs=[pl.BlockSpec(memory_space=pltpu.HBM)] * 5,
        out_specs=pl.BlockSpec(memory_space=pl.ANY),
        scratch_shapes=[
            pltpu.VMEM(volume.shape, bf16),
            pltpu.VMEM(kernel_one.shape, bf16),
            pltpu.VMEM(kernel_two.shape, bf16),
            pltpu.VMEM((1, chans), jnp.float32),
            pltpu.VMEM((1, chans), jnp.float32),
            packed,
            packed,
            pltpu.VMEM((4, 4, width, chans), bf16),
            pltpu.VMEM((4, 4, width, chans), bf16),
            packed,
            dma((6,)), dma((4,)), dma((4,)), dma((8,)), dma((8,)), dma((8,)), dma((8,)), dma((4,)), dma((4,)),
        ],
        compiler_params=pltpu.CompilerParams(
            collective_id=0, has_side_effects=True, vmem_limit_bytes=67_043_328),
    )(volume, kernel_one, bias_one.reshape(1, chans), kernel_two, bias_two.reshape(1, chans))
    parts = parts.reshape(2, 2, 2, width, 2, shard)
    return parts.transpose(0, 2, 1, 4, 3, 5).reshape(4, 4, width, shard)


def solution(mesh):
    in_specs = (P("depth", "height", None, "filt"), P(), P(), P(), P())
    out_specs = P("depth", "height", None, "filt")
    step = functools.partial(body, mesh.shape["depth"], mesh.shape["height"])
    return jax.shard_map(step, mesh=mesh, in_specs=in_specs, out_specs=out_specs, check_vma=False)
```

time: 134 us -> 32.6 us (0.24)
  the two profiles are of different devices: /device:TPU:86 before, /device:TPU:541 now
where the time goes in v1:
time: 32.6 us; the launch traced here: 32.4 us
  Pallas kernels  30.6 us (94%)
  local copies, waits for them, and re-layouts  1.8 us (6%)
    pallas_call x1, Pallas kernels, body(): pl.pallas_call(functools.partial(kernel, depths, heights), out_shape=jax....  30.6 us
    reshape x1, local copies, waits for them, and re-layouts, body(): parts = parts.reshape(2, 2, 2, width, 2, shard)  1.04 us
    transpose x1, local copies, waits for them, and re-layouts, body(): return parts.transpose(0, 2, 1, 4, 3, 5).reshape(4, 4, width, shard)  0.76 us

profile of v1, /device:TPU:541, one launch (start us, length us, event | category | flops | bytes accessed | tf_op | source)
XLA Modules:
  0.0 32.4 jit_solution(8604107807065214573)
XLA Ops:
  0.0 30.6 %shard_map.55 = bf16[4,2,64,128]{3,2,1,0:T(8,128)(2,1)} custom-call(bf16[4,4,64,64]{3,2,1,0:T(8,128)(2,1)} %vol.1, bf16[3,3,3,256,256]{4,3,2,1,0:T(8,128)(2,1)} %k1.1, f32[1,256]{1,0:T(1,128)} %bitcast.7, bf16[3,3,3,256,256]{4,3,2,1,0:T(8,128)(2,1)} %k2.1, f32[1,256]{1,0:T(1,128)} %bitcast.8), custom_call_target="tpu_custom_call" | custom-call | tf_op jit(solution)/shard_map/pallas_call | solution.py:222
  30.6 1.0 %reshape.14 = bf16[2,2,2,64,2,64]{5,4,3,2,1,0:T(2,128)(2,1)S(1)} reshape(bf16[4,2,64,128]{3,2,1,0:T(8,128)(2,1)} %shard_map.55) | data formatting | bytes 262144 | tf_op jit(solution)/shard_map/reshape | solution.py:243
  31.7 0.8 %copy.6 = bf16[2,2,2,2,64,64]{5,4,3,2,1,0:T(8,128)(2,1)} copy(bf16[2,2,2,2,64,64]{5,3,4,1,2,0:T(2,128)(2,1)S(1)} %bitcast.6) | data formatting | bytes 262144 | tf_op jit(solution)/shard_map/transpose | solution.py:244

commit v2 on v0

v2 whole, which is shorter than its diff:
```python
import functools

import jax
import jax.numpy as jnp
from jax import lax
from jax.experimental import pallas as pl
from jax.experimental.pallas import tpu as pltpu
from jax.sharding import PartitionSpec as P

MESH = pl.DeviceIdType.MESH
VMEM_LIMIT = 67_043_328
MESSAGES = (
    (0, -1, 1), (0, 1, 1), (0, -1, 2), (0, 1, 2),
    (-1, -1, 1), (-1, 1, 1), (-1, 0, 1),
    (1, -1, 2), (1, 1, 2), (1, 0, 2),
)
SIDES, UPPER, LOWER = (0, 1, 2, 3), (4, 5, 6), (7, 8, 9)
STEPS = tuple((a, b) for a in (-1, 0, 1) for b in (-1, 0, 1) if (a, b) != (0, 0))


def opposite(m):
    sd, sh, row = MESSAGES[m]
    return MESSAGES.index((-sd, -sh, row if sd == 0 else 3 - row))


def edge_of(m):
    sd, sh, row = MESSAGES[m]
    return pl.ds(row, 1), pl.ds(1 if sh <= 0 else 2, 2 if sh == 0 else 1)


def halo_of(m):
    sd, sh, row = MESSAGES[m]
    return pl.ds({-1: 0, 0: row, 1: 3}[sd], 1), pl.ds({-1: 0, 0: 1, 1: 3}[sh], 2 if sh == 0 else 1)


def flip_of(d):
    return (d % 2) * (1 - (d % 4) // 2)


def leaky(value):
    return jnp.where(value > 0, value, 0.3 * value)


def taps(x, w, rows, count, a, c):
    width, chans = x.shape[2], x.shape[3]
    total = None
    for b in range(3):
        lhs = x[rows : rows + count, b : b + 2].reshape(count * 2 * width, chans)
        part = jnp.dot(lhs, w[a, b, c], preferred_element_type=jnp.float32)
        total = part if total is None else total + part
    return total


def inner_taps(x, w, acc):
    half = 2 * x.shape[2]
    for c in range(3):
        both = taps(x, w, 1, 2, 1, c)
        acc[c, 0] = both[:half] + taps(x, w, 2, 1, 2, c)
        acc[c, 1] = both[half:] + taps(x, w, 1, 1, 0, c)


def outer_taps(x, w, acc, bias, row):
    width, chans = x.shape[2], x.shape[3]
    rows = 2 * width
    low, centre, high = (acc[c, row] + taps(x, w, 3 * row, 1, 2 * row, c) for c in range(3))
    w_of = lax.rem(lax.broadcasted_iota(jnp.int32, (rows, chans), 0), width)
    low = jnp.where(w_of == 0, 0.0, pltpu.roll(low, 1, 0))
    high = jnp.where(w_of == width - 1, 0.0, pltpu.roll(high, rows - 1, 0))
    return leaky(low + centre + high + bias[...]).astype(jnp.bfloat16)


def kernel(
    depths, heights,
    vol, k1, b1, k2, b2, out,
    xv, w1, w2, bb1, bb2, xs, ra, xh, hh, os, ro, acc,
    lsem, sa, qa, sb, qb, sc, qc, se, qe,
):
    d, h, f = lax.axis_index("depth"), lax.axis_index("height"), lax.axis_index("filt")
    flip = flip_of(d)
    width, shard = vol.shape[2], vol.shape[3]

    def quarter_of(g):
        return 2 * ((g // 2 + flip) % 2) + g % 2

    quarter = quarter_of(f)
    peers = [(f + r) % 4 for r in (2, 3, 1)]
    fine_d, fine_h = 2 * d + quarter // 2, 2 * h + f % 2
    has = {
        -1: (fine_d > 0, fine_h > 0),
        0: (True, True),
        1: (fine_d < 2 * depths - 1, fine_h < 2 * heights - 1),
    }

    def neighbour(sd, sh):
        nd, nh = fine_d + sd, fine_h + sh
        block = nd // 2
        nf = 2 * ((nd + flip_of(block)) % 2) + nh % 2
        if sd == 0:
            valid = has[sh][1]
        else:
            valid = has[sd][0] if sh == 0 else has[sd][0] & has[sh][1]
        return valid, {"depth": block, "height": nh // 2, "filt": nf}

    loads = [
        pltpu.make_async_copy(src, dst, lsem.at[i])
        for i, (src, dst) in enumerate(((vol, xv), (b1, bb1), (b2, bb2), (k1, w1), (k2, w2)))
    ]
    loads[0].start()
    barrier = pltpu.get_barrier_semaphore()
    for step in STEPS:
        valid, device = neighbour(*step)

        @pl.when(valid)
        def _():
            pl.semaphore_signal(barrier, inc=1, device_id=device, device_id_type=MESH)

    for load in loads[1:]:
        load.start()
    loads[0].wait()
    for q in range(4):
        top, side = 2 * (q // 2), 2 * (q % 2)
        xs[q] = jnp.concatenate([xv[top : top + 2, side], xv[top : top + 2, side + 1]], axis=-1)

    for m in range(len(MESSAGES)):
        valid, _ = neighbour(*MESSAGES[m][:2])

        @pl.when(jnp.logical_not(valid))
        def _():
            for ref in (xh, hh):
                ref[halo_of(m)] = jnp.zeros_like(ref[halo_of(m)])

    tall = 3 - jnp.where(fine_d == 0, 1, 0) - jnp.where(fine_d == 2 * depths - 1, 1, 0)
    wide = 3 - jnp.where(fine_h == 0, 1, 0) - jnp.where(fine_h == 2 * heights - 1, 1, 0)
    pl.semaphore_wait(barrier, tall * wide - 1)

    def gather(g):
        return pltpu.make_async_remote_copy(
            src_ref=xs.at[quarter_of(g)], dst_ref=ra.at[f], send_sem=sa.at[g], recv_sem=qa.at[f],
            device_id={"filt": g}, device_id_type=MESH)

    def gathered(g):
        return pltpu.make_async_remote_copy(
            src_ref=xs.at[quarter], dst_ref=ra.at[g], send_sem=sa.at[g], recv_sem=qa.at[g],
            device_id={"filt": g}, device_id_type=MESH)

    for g in peers:
        gather(g).start()
    ra[f] = xs[quarter]
    for g in reversed(peers):
        gathered(g).wait_recv()
    for i in range(2):
        for j in range(2):
            xh[1 + i, 1 + j] = jnp.concatenate(
                [ra[g, i, :, j * shard : (j + 1) * shard] for g in range(4)], axis=-1)

    def halo(ref, send, recv, m):
        valid, device = neighbour(*MESSAGES[m][:2])

        def copy():
            return pltpu.make_async_remote_copy(
                src_ref=ref.at[edge_of(m)], dst_ref=ref.at[halo_of(opposite(m))],
                send_sem=send.at[m], recv_sem=recv.at[opposite(m)],
                device_id=device, device_id_type=MESH)

        def arrival():
            return pltpu.make_async_remote_copy(
                src_ref=ref.at[edge_of(m)], dst_ref=ref.at[halo_of(m)],
                send_sem=send.at[m], recv_sem=recv.at[m],
                device_id=device, device_id_type=MESH)

        return valid, copy, arrival

    def start(ref, send, recv, messages):
        for m in messages:
            valid, copy, _ = halo(ref, send, recv, m)

            @pl.when(valid)
            def _():
                copy().start()

    def finish(ref, send, recv, messages):
        for m in messages:
            valid, _, arrival = halo(ref, send, recv, m)

            @pl.when(valid)
            def _():
                arrival().wait_recv()

    start(xh, sb, qb, SIDES + UPPER + LOWER)
    loads[1].wait()
    loads[3].wait()
    finish(xh, sb, qb, SIDES)
    inner_taps(xh, w1, acc)
    for row, messages in ((0, UPPER), (1, LOWER)):
        finish(xh, sb, qb, messages)
        hh[1 + row, 1:3] = outer_taps(xh, w1, acc, bb1, row).reshape(2, width, 4 * shard)
        start(hh, sc, qc, SIDES[2 * row : 2 * row + 2] + messages)

    loads[2].wait()
    loads[4].wait()
    finish(hh, sc, qc, SIDES)
    inner_taps(hh, w2, acc)

    def scatter(g, row):
        return pltpu.make_async_remote_copy(
            src_ref=os.at[g, row], dst_ref=ro.at[quarter, row],
            send_sem=se.at[g, row], recv_sem=qe.at[quarter, row],
            device_id={"filt": g}, device_id_type=MESH)

    def scattered(g, row):
        q = quarter_of(g)
        return pltpu.make_async_remote_copy(
            src_ref=os.at[g, row], dst_ref=ro.at[q, row],
            send_sem=se.at[g, row], recv_sem=qe.at[q, row],
            device_id={"filt": g}, device_id_type=MESH)

    for row, messages in ((0, UPPER), (1, LOWER)):
        finish(hh, sc, qc, messages)
        result = outer_taps(hh, w2, acc, bb2, row)
        for g in range(4):
            part = result[:, g * shard : (g + 1) * shard]
            os[g, row] = jnp.concatenate([part[:width], part[width:]], axis=-1)
        for g in peers:
            scatter(g, row).start()
        ro[quarter, row] = os[f, row]

    for g in peers:
        gather(g).wait_send()
    for refs in ((xh, sb, qb), (hh, sc, qc)):
        for m in range(len(MESSAGES)):
            valid, copy, _ = halo(*refs, m)

            @pl.when(valid)
            def _():
                copy().wait_send()

    for row in range(2):
        for g in reversed(peers):
            scattered(g, row).wait_recv()
        for q in range(4):
            for j in range(2):
                out[2 * (q // 2) + row, 2 * (q % 2) + j] = ro[q, row, :, j * shard : (j + 1) * shard]
    for row in range(2):
        for g in peers:
            scatter(g, row).wait_send()


def body(depths, heights, volume, kernel_one, bias_one, kernel_two, bias_two):
    _, _, width, shard = volume.shape
    chans = 4 * shard
    bf16, dma = jnp.bfloat16, pltpu.SemaphoreType.DMA
    packed = pltpu.VMEM((4, 2, width, 2 * shard), bf16)
    padded = pltpu.VMEM((4, 4, width, chans), bf16)
    bias = pltpu.VMEM((1, chans), jnp.float32)
    return pl.pallas_call(
        functools.partial(kernel, depths, heights),
        out_shape=jax.ShapeDtypeStruct(volume.shape, bf16),
        in_specs=[pl.BlockSpec(memory_space=pl.ANY)] * 5,
        out_specs=pl.BlockSpec(memory_space=pltpu.VMEM),
        scratch_shapes=[
            pltpu.VMEM(volume.shape, bf16),
            pltpu.VMEM(kernel_one.shape, bf16),
            pltpu.VMEM(kernel_two.shape, bf16),
            bias,
            bias,
            packed,
            packed,
            padded,
            padded,
            packed,
            packed,
            pltpu.VMEM((3, 2, 2 * width, chans), jnp.float32),
            dma((5,)), dma((4,)), dma((4,)), dma((10,)), dma((10,)), dma((10,)), dma((10,)), dma((4, 2)), dma((4, 2)),
        ],
        compiler_params=pltpu.CompilerParams(
            collective_id=0, has_side_effects=True, vmem_limit_bytes=VMEM_LIMIT),
    )(volume, kernel_one, bias_one.reshape(1, chans), kernel_two, bias_two.reshape(1, chans))


def solution(mesh):
    in_specs = (P("depth", "height", None, "filt"), P(), P(), P(), P())
    out_specs = P("depth", "height", None, "filt")
    step = functools.partial(body, mesh.shape["depth"], mesh.shape["height"])
    return jax.shard_map(step, mesh=mesh, in_specs=in_specs, out_specs=out_specs, check_vma=False)
```

time: 134 us -> 30.7 us (0.23)
  the two profiles are of different devices: /device:TPU:86 before, /device:TPU:1 now
where the time goes in v2:
time: 30.7 us; the launch traced here: 30.5 us
  Pallas kernels  28.8 us (94%)
  local copies, waits for them, and re-layouts  1.67 us (5%)
    pallas_call x1, Pallas kernels, body(): pl.pallas_call(functools.partial(kernel, depths, heights), out_shape=jax....  28.8 us
    unnamed x1, local copies, waits for them, and re-layouts  1.67 us

profile of v2, /device:TPU:1, one launch (start us, length us, event | category | flops | bytes accessed | tf_op | source)
XLA Modules:
  0.0 30.5 jit_solution(17958998059131676315)
XLA Ops:
  0.0 28.8 %shard_map.55 = bf16[4,4,64,64]{3,2,1,0:T(8,128)(2,1)} custom-call(bf16[4,4,64,64]{3,2,1,0:T(8,128)(2,1)} %vol.1, bf16[3,3,3,256,256]{4,3,2,1,0:T(8,128)(2,1)} %k1.1, f32[1,256]{1,0:T(1,128)} %bitcast.2, bf16[3,3,3,256,256]{4,3,2,1,0:T(8,128)(2,1)} %k2.1, f32[1,256]{1,0:T(1,128)} %bitcast.3), custom_call_target="tpu_custom_call" | custom-call | tf_op jit(solution)/shard_map/pallas_call | solution.py:255
  28.8 1.7 %copy.7 = bf16[4,4,64,64]{3,2,1,0:T(8,128)(2,1)} copy(bf16[4,4,64,64]{3,2,1,0:T(8,128)(2,1)} %shard_map.55) | data formatting | bytes 262144

commit v3 on v2

--- a/solution.py
+++ b/solution.py
@@ -8,29 +8,9 @@
 from jax.sharding import PartitionSpec as P
 
 MESH = pl.DeviceIdType.MESH
-VMEM_LIMIT = 67_043_328
-MESSAGES = (
-    (0, -1, 1), (0, 1, 1), (0, -1, 2), (0, 1, 2),
-    (-1, -1, 1), (-1, 1, 1), (-1, 0, 1),
-    (1, -1, 2), (1, 1, 2), (1, 0, 2),
-)
-SIDES, UPPER, LOWER = (0, 1, 2, 3), (4, 5, 6), (7, 8, 9)
+VMEM_LIMIT = 40_000_000
 STEPS = tuple((a, b) for a in (-1, 0, 1) for b in (-1, 0, 1) if (a, b) != (0, 0))
-
-
-def opposite(m):
-    sd, sh, row = MESSAGES[m]
-    return MESSAGES.index((-sd, -sh, row if sd == 0 else 3 - row))
-
-
-def edge_of(m):
-    sd, sh, row = MESSAGES[m]
-    return pl.ds(row, 1), pl.ds(1 if sh <= 0 else 2, 2 if sh == 0 else 1)
-
-
-def halo_of(m):
-    sd, sh, row = MESSAGES[m]
-    return pl.ds({-1: 0, 0: row, 1: 3}[sd], 1), pl.ds({-1: 0, 0: 1, 1: 3}[sh], 2 if sh == 0 else 1)
+NEAR, FAR, FACE, CORNER, FORWARD = (range(2 * i, 2 * i + 2) for i in range(5))
 
 
 def flip_of(d):
@@ -85,20 +65,11 @@
     quarter = quarter_of(f)
     peers = [(f + r) % 4 for r in (2, 3, 1)]
     fine_d, fine_h = 2 * d + quarter // 2, 2 * h + f % 2
-    has = {
-        -1: (fine_d > 0, fine_h > 0),
-        0: (True, True),
-        1: (fine_d < 2 * depths - 1, fine_h < 2 * heights - 1),
-    }
-
     def neighbour(sd, sh):
         nd, nh = fine_d + sd, fine_h + sh
         block = nd // 2
         nf = 2 * ((nd + flip_of(block)) % 2) + nh % 2
-        if sd == 0:
-            valid = has[sh][1]
-        else:
-            valid = has[sd][0] if sh == 0 else has[sd][0] & has[sh][1]
+        valid = (nd >= 0) & (nd < 2 * depths) & (nh >= 0) & (nh < 2 * heights)
         return valid, {"depth": block, "height": nh // 2, "filt": nf}
 
     loads = [
@@ -121,13 +92,23 @@
         top, side = 2 * (q // 2), 2 * (q % 2)
         xs[q] = jnp.concatenate([xv[top : top + 2, side], xv[top : top + 2, side + 1]], axis=-1)
 
-    for m in range(len(MESSAGES)):
-        valid, _ = neighbour(*MESSAGES[m][:2])
-
-        @pl.when(jnp.logical_not(valid))
+    core = f % 2
+    outward = 2 * core - 1
+    near_edge, near_halo = 2 - core, 3 - 3 * core
+    far_edge, far_halo = 1 + core, 3 * core
+    has_far = (fine_h + outward >= 0) & (fine_h + outward < 2 * heights)
+    has_depth = (fine_d > 0, fine_d < 2 * depths - 1)
+
+    for ref in (xh, hh):
+        @pl.when(jnp.logical_not(has_far))
         def _():
-            for ref in (xh, hh):
-                ref[halo_of(m)] = jnp.zeros_like(ref[halo_of(m)])
+            for row in range(4):
+                ref[row, far_halo] = jnp.zeros_like(ref[row, far_halo])
+
+        for i in range(2):
+            @pl.when(jnp.logical_not(has_depth[i]))
+            def _():
+                ref[3 * i] = jnp.zeros_like(ref[3 * i])
 
     tall = 3 - jnp.where(fine_d == 0, 1, 0) - jnp.where(fine_d == 2 * depths - 1, 1, 0)
     wide = 3 - jnp.where(fine_h == 0, 1, 0) - jnp.where(fine_h == 2 * heights - 1, 1, 0)
@@ -154,52 +135,82 @@
                 [ra[g, i, :, j * shard : (j + 1) * shard] for g in range(4)], axis=-1)
 
     def halo(ref, send, recv, m):
-        valid, device = neighbour(*MESSAGES[m][:2])
+        i, whole = m % 2, pl.ds(1, 2)
+        if m in NEAR:
+            valid, to, step = None, m, (0, -outward)
+            edge, there, here = (1 + i, near_edge), (1 + i, 3 * core), (1 + i, near_halo)
+        elif m in FAR:
+            valid, to, step = has_far, m, (0, outward)
+            edge, there, here = (1 + i, far_edge), (1 + i, 3 - 3 * core), (1 + i, far_halo)
+        elif m in FACE:
+            valid, to, step = has_depth[i], FACE[1 - i], (2 * i - 1, 0)
+            edge, there, here = (1 + i, whole), (3 - 3 * i, whole), (3 * i, whole)
+        elif m in CORNER:
+            valid, to, step = has_depth[i] & has_far, CORNER[1 - i], (2 * i - 1, outward)
+            edge, there, here = (1 + i, far_edge), (3 - 3 * i, 3 - 3 * core), (3 * i, far_halo)
+        else:
+            valid, to, step = has_depth[i], m, (0, -outward)
+            edge, there, here = (3 * i, near_edge), (3 * i, 3 * core), (3 * i, near_halo)
+        _, device = neighbour(*step)
 
         def copy():
             return pltpu.make_async_remote_copy(
-                src_ref=ref.at[edge_of(m)], dst_ref=ref.at[halo_of(opposite(m))],
-                send_sem=send.at[m], recv_sem=recv.at[opposite(m)],
+                src_ref=ref.at[edge], dst_ref=ref.at[there],
+                send_sem=send.at[m], recv_sem=recv.at[to],
                 device_id=device, device_id_type=MESH)
 
         def arrival():
             return pltpu.make_async_remote_copy(
-                src_ref=ref.at[edge_of(m)], dst_ref=ref.at[halo_of(m)],
+                src_ref=ref.at[edge], dst_ref=ref.at[here],
                 send_sem=send.at[m], recv_sem=recv.at[m],
                 device_id=device, device_id_type=MESH)
 
         return valid, copy, arrival
 
-    def start(ref, send, recv, messages):
+    def when(valid, act):
+        if valid is None:
+            act()
+        else:
+            pl.when(valid)(act)
+
+    def start(refs, *messages):
         for m in messages:
-            valid, copy, _ = halo(ref, send, recv, m)
-
-            @pl.when(valid)
-            def _():
-                copy().start()
-
-    def finish(ref, send, recv, messages):
+            valid, copy, _ = halo(*refs, m)
+            when(valid, lambda: copy().start())
+
+    def finish(refs, *messages):
         for m in messages:
-            valid, _, arrival = halo(ref, send, recv, m)
-
-            @pl.when(valid)
-            def _():
-                arrival().wait_recv()
-
-    start(xh, sb, qb, SIDES + UPPER + LOWER)
+            valid, _, arrival = halo(*refs, m)
+            when(valid, lambda: arrival().wait_recv())
+
+    def forward(refs, i):
+        valid, _, arrival = halo(*refs, FACE[i])
+        _, copy, _ = halo(*refs, FORWARD[i])
+
+        @pl.when(valid)
+        def _():
+            arrival().wait_recv()
+            copy().start()
+
+    first, second = (xh, sb, qb), (hh, sc, qc)
+    start(first, *FACE, *FAR, *CORNER, *NEAR)
     loads[1].wait()
     loads[3].wait()
-    finish(xh, sb, qb, SIDES)
+    finish(first, *NEAR, *FAR)
     inner_taps(xh, w1, acc)
-    for row, messages in ((0, UPPER), (1, LOWER)):
-        finish(xh, sb, qb, messages)
+    forward(first, 0)
+    forward(first, 1)
+    for row in range(2):
+        finish(first, CORNER[row], FORWARD[row])
         hh[1 + row, 1:3] = outer_taps(xh, w1, acc, bb1, row).reshape(2, width, 4 * shard)
-        start(hh, sc, qc, SIDES[2 * row : 2 * row + 2] + messages)
+        start(second, FACE[row], FAR[row], CORNER[row], NEAR[row])
 
     loads[2].wait()
     loads[4].wait()
-    finish(hh, sc, qc, SIDES)
+    finish(second, *NEAR, *FAR)
     inner_taps(hh, w2, acc)
+    forward(second, 0)
+    forward(second, 1)
 
     def scatter(g, row):
         return pltpu.make_async_remote_copy(
@@ -214,8 +225,8 @@
             send_sem=se.at[g, row], recv_sem=qe.at[q, row],
             device_id={"filt": g}, device_id_type=MESH)
 
-    for row, messages in ((0, UPPER), (1, LOWER)):
-        finish(hh, sc, qc, messages)
+    for row in range(2):
+        finish(second, CORNER[row], FORWARD[row])
         result = outer_taps(hh, w2, acc, bb2, row)
         for g in range(4):
             part = result[:, g * shard : (g + 1) * shard]
@@ -226,13 +237,10 @@
 
     for g in peers:
         gather(g).wait_send()
-    for refs in ((xh, sb, qb), (hh, sc, qc)):
-        for m in range(len(MESSAGES)):
+    for refs in (first, second):
+        for m in range(10):
             valid, copy, _ = halo(*refs, m)
-
-            @pl.when(valid)
-            def _():
-                copy().wait_send()
+            when(valid, lambda: copy().wait_send())
 
     for row in range(2):
         for g in reversed(peers):
@@ -255,7 +263,7 @@
     return pl.pallas_call(
         functools.partial(kernel, depths, heights),
         out_shape=jax.ShapeDtypeStruct(volume.shape, bf16),
-        in_specs=[pl.BlockSpec(memory_space=pl.ANY)] * 5,
+        in_specs=[pl.BlockSpec(memory_space=pltpu.HBM)] * 5,
         out_specs=pl.BlockSpec(memory_space=pltpu.VMEM),
         scratch_shapes=[
             pltpu.VMEM(volume.shape, bf16),
@@ -274,7 +282,7 @@
         ],
         compiler_params=pltpu.CompilerParams(
             collective_id=0, has_side_effects=True, vmem_limit_bytes=VMEM_LIMIT),
-    )(volume, kernel_one, bias_one.reshape(1, chans), kernel_two, bias_two.reshape(1, chans))
+    )(*(pltpu.with_memory_space_constraint(v, pltpu.HBM) for v in (volume, kernel_one, bias_one.reshape(1, chans), kernel_two, bias_two.reshape(1, chans))))
 
 
 def solution(mesh):

time: 30.7 us -> 29.7 us (0.967)
  local copies, waits for them, and re-layouts: 1.67 us -> 0.71 us
    unnamed x1, local copies, waits for them, and re-layouts: 1.67 us -> 0.71 us
where the time goes in v3:
time: 29.7 us; the launch traced here: 29.6 us
  Pallas kernels  28.9 us (97%)
  local copies, waits for them, and re-layouts  0.71 us (2%)
    pallas_call x1, Pallas kernels, body(): pl.pallas_call(functools.partial(kernel, depths, heights), out_shape=jax....  28.9 us
    unnamed x1, local copies, waits for them, and re-layouts  0.71 us

profile of v3, /device:TPU:1, one launch (start us, length us, event | category | flops | bytes accessed | tf_op | source)
XLA Modules:
  0.0 29.6 jit_solution(7512860724693190753)
XLA Ops:
  0.0 28.9 %shard_map.55 = bf16[4,4,64,64]{3,2,1,0:T(8,128)(2,1)S(1)} custom-call(bf16[4,4,64,64]{3,2,1,0:T(8,128)(2,1)} %vol.1, bf16[3,3,3,256,256]{4,3,2,1,0:T(8,128)(2,1)} %k1.1, f32[1,256]{1,0:T(1,128)} %bitcast.2, bf16[3,3,3,256,256]{4,3,2,1,0:T(8,128)(2,1)} %k2.1, f32[1,256]{1,0:T(1,128)} %bitcast.3), custom_call_target="tpu_custom_call" | custom-call | tf_op jit(solution)/shard_map/pallas_call | solution.py:263
  28.9 0.7 %copy.7 = bf16[4,4,64,64]{3,2,1,0:T(8,128)(2,1)} copy(bf16[4,4,64,64]{3,2,1,0:T(8,128)(2,1)S(1)} %shard_map.55) | data formatting | bytes 262144

commit v4 on v3

--- a/solution.py
+++ b/solution.py
@@ -10,7 +10,7 @@
 MESH = pl.DeviceIdType.MESH
 VMEM_LIMIT = 40_000_000
 STEPS = tuple((a, b) for a in (-1, 0, 1) for b in (-1, 0, 1) if (a, b) != (0, 0))
-NEAR, FAR, FACE, CORNER, FORWARD = (range(2 * i, 2 * i + 2) for i in range(5))
+NEAR, FAR, FACE, REST, CORNER, FORWARD = (range(2 * i, 2 * i + 2) for i in range(6))
 
 
 def flip_of(d):
@@ -135,7 +135,7 @@
                 [ra[g, i, :, j * shard : (j + 1) * shard] for g in range(4)], axis=-1)
 
     def halo(ref, send, recv, m):
-        i, whole = m % 2, pl.ds(1, 2)
+        i = m % 2
         if m in NEAR:
             valid, to, step = None, m, (0, -outward)
             edge, there, here = (1 + i, near_edge), (1 + i, 3 * core), (1 + i, near_halo)
@@ -144,7 +144,10 @@
             edge, there, here = (1 + i, far_edge), (1 + i, 3 - 3 * core), (1 + i, far_halo)
         elif m in FACE:
             valid, to, step = has_depth[i], FACE[1 - i], (2 * i - 1, 0)
-            edge, there, here = (1 + i, whole), (3 - 3 * i, whole), (3 * i, whole)
+            edge, there, here = (1 + i, near_edge), (3 - 3 * i, near_edge), (3 * i, near_edge)
+        elif m in REST:
+            valid, to, step = has_depth[i], REST[1 - i], (2 * i - 1, 0)
+            edge, there, here = (1 + i, far_edge), (3 - 3 * i, far_edge), (3 * i, far_edge)
         elif m in CORNER:
             valid, to, step = has_depth[i] & has_far, CORNER[1 - i], (2 * i - 1, outward)
             edge, there, here = (1 + i, far_edge), (3 - 3 * i, 3 - 3 * core), (3 * i, far_halo)
@@ -193,24 +196,24 @@
             copy().start()
 
     first, second = (xh, sb, qb), (hh, sc, qc)
-    start(first, *FACE, *FAR, *CORNER, *NEAR)
+    start(first, *FACE, *FAR, *CORNER, *REST, *NEAR)
     loads[1].wait()
     loads[3].wait()
+    forward(first, 0)
+    forward(first, 1)
     finish(first, *NEAR, *FAR)
     inner_taps(xh, w1, acc)
-    forward(first, 0)
-    forward(first, 1)
-    for row in range(2):
-        finish(first, CORNER[row], FORWARD[row])
+    for row in range(2):
+        finish(first, FORWARD[row], CORNER[row], REST[row])
         hh[1 + row, 1:3] = outer_taps(xh, w1, acc, bb1, row).reshape(2, width, 4 * shard)
-        start(second, FACE[row], FAR[row], CORNER[row], NEAR[row])
+        start(second, FACE[row], FAR[row], CORNER[row], REST[row], NEAR[row])
 
     loads[2].wait()
     loads[4].wait()
+    forward(second, 0)
+    forward(second, 1)
     finish(second, *NEAR, *FAR)
     inner_taps(hh, w2, acc)
-    forward(second, 0)
-    forward(second, 1)
 
     def scatter(g, row):
         return pltpu.make_async_remote_copy(
@@ -226,7 +229,7 @@
             device_id={"filt": g}, device_id_type=MESH)
 
     for row in range(2):
-        finish(second, CORNER[row], FORWARD[row])
+        finish(second, FORWARD[row], CORNER[row], REST[row])
         result = outer_taps(hh, w2, acc, bb2, row)
         for g in range(4):
             part = result[:, g * shard : (g + 1) * shard]
@@ -238,7 +241,7 @@
     for g in peers:
         gather(g).wait_send()
     for refs in (first, second):
-        for m in range(10):
+        for m in range(12):
             valid, copy, _ = halo(*refs, m)
             when(valid, lambda: copy().wait_send())
 
@@ -278,7 +281,7 @@
             packed,
             packed,
             pltpu.VMEM((3, 2, 2 * width, chans), jnp.float32),
-            dma((5,)), dma((4,)), dma((4,)), dma((10,)), dma((10,)), dma((10,)), dma((10,)), dma((4, 2)), dma((4, 2)),
+            dma((5,)), dma((4,)), dma((4,)), dma((12,)), dma((12,)), dma((12,)), dma((12,)), dma((4, 2)), dma((4, 2)),
         ],
         compiler_params=pltpu.CompilerParams(
             collective_id=0, has_side_effects=True, vmem_limit_bytes=VMEM_LIMIT),

time: 29.7 us -> 28.9 us (0.973)
  Pallas kernels: 28.9 us -> 28.1 us
    pallas_call x1, Pallas kernels: 28.9 us -> 28.1 us  [body(): pl.pallas_call(functools.partial(kernel, depths, heights), out_shape=jax....]
where the time goes in v4:
time: 28.9 us; the launch traced here: 28.8 us
  Pallas kernels  28.1 us (97%)
  local copies, waits for them, and re-layouts  0.71 us (2%)
    pallas_call x1, Pallas kernels, body(): pl.pallas_call(functools.partial(kernel, depths, heights), out_shape=jax....  28.1 us
    unnamed x1, local copies, waits for them, and re-layouts  0.71 us

profile of v4, /device:TPU:1, one launch (start us, length us, event | category | flops | bytes accessed | tf_op | source)
XLA Modules:
  0.0 28.8 jit_solution(10232556719573200247)
XLA Ops:
  0.0 28.1 %shard_map.55 = bf16[4,4,64,64]{3,2,1,0:T(8,128)(2,1)S(1)} custom-call(bf16[4,4,64,64]{3,2,1,0:T(8,128)(2,1)} %vol.1, bf16[3,3,3,256,256]{4,3,2,1,0:T(8,128)(2,1)} %k1.1, f32[1,256]{1,0:T(1,128)} %bitcast.2, bf16[3,3,3,256,256]{4,3,2,1,0:T(8,128)(2,1)} %k2.1, f32[1,256]{1,0:T(1,128)} %bitcast.3), custom_call_target="tpu_custom_call" | custom-call | tf_op jit(solution)/shard_map/pallas_call | solution.py:266
  28.1 0.7 %copy.7 = bf16[4,4,64,64]{3,2,1,0:T(8,128)(2,1)} copy(bf16[4,4,64,64]{3,2,1,0:T(8,128)(2,1)S(1)} %shard_map.55) | data formatting | bytes 262144

commit v5 on v4

--- a/solution.py
+++ b/solution.py
@@ -85,8 +85,6 @@
         def _():
             pl.semaphore_signal(barrier, inc=1, device_id=device, device_id_type=MESH)
 
-    for load in loads[1:]:
-        load.start()
     loads[0].wait()
     for q in range(4):
         top, side = 2 * (q // 2), 2 * (q % 2)
@@ -126,6 +124,8 @@
 
     for g in peers:
         gather(g).start()
+    for load in loads[1:4]:
+        load.start()
     ra[f] = xs[quarter]
     for g in reversed(peers):
         gathered(g).wait_recv()
@@ -197,6 +197,7 @@
 
     first, second = (xh, sb, qb), (hh, sc, qc)
     start(first, *FACE, *FAR, *CORNER, *REST, *NEAR)
+    loads[4].start()
     loads[1].wait()
     loads[3].wait()
     forward(first, 0)

time: 28.9 us -> 29 us (level)
  no operation moved by 1% of the time
where the time goes in v5:
time: 29 us; the launch traced here: 28.8 us
  Pallas kernels  28.1 us (97%)
  local copies, waits for them, and re-layouts  0.71 us (2%)
    pallas_call x1, Pallas kernels, body(): pl.pallas_call(functools.partial(kernel, depths, heights), out_shape=jax....  28.1 us
    unnamed x1, local copies, waits for them, and re-layouts  0.71 us

profile of v5, /device:TPU:1, one launch (start us, length us, event | category | flops | bytes accessed | tf_op | source)
XLA Modules:
  0.0 28.8 jit_solution(7495671638185454528)
XLA Ops:
  0.0 28.1 %shard_map.55 = bf16[4,4,64,64]{3,2,1,0:T(8,128)(2,1)S(1)} custom-call(bf16[4,4,64,64]{3,2,1,0:T(8,128)(2,1)} %vol.1, bf16[3,3,3,256,256]{4,3,2,1,0:T(8,128)(2,1)} %k1.1, f32[1,256]{1,0:T(1,128)} %bitcast.2, bf16[3,3,3,256,256]{4,3,2,1,0:T(8,128)(2,1)} %k2.1, f32[1,256]{1,0:T(1,128)} %bitcast.3), custom_call_target="tpu_custom_call" | custom-call | tf_op jit(solution)/shard_map/pallas_call | solution.py:267
  28.1 0.7 %copy.7 = bf16[4,4,64,64]{3,2,1,0:T(8,128)(2,1)} copy(bf16[4,4,64,64]{3,2,1,0:T(8,128)(2,1)S(1)} %shard_map.55) | data formatting | bytes 262144

commit v6 on v4

--- a/solution.py
+++ b/solution.py
@@ -10,7 +10,7 @@
 MESH = pl.DeviceIdType.MESH
 VMEM_LIMIT = 40_000_000
 STEPS = tuple((a, b) for a in (-1, 0, 1) for b in (-1, 0, 1) if (a, b) != (0, 0))
-NEAR, FAR, FACE, REST, CORNER, FORWARD = (range(2 * i, 2 * i + 2) for i in range(6))
+NEAR, FAR, FACE, REST, CORNER, FORWARD = range(6)
 
 
 def flip_of(d):
@@ -25,7 +25,7 @@
     width, chans = x.shape[2], x.shape[3]
     total = None
     for b in range(3):
-        lhs = x[rows : rows + count, b : b + 2].reshape(count * 2 * width, chans)
+        lhs = x[pl.ds(rows, count), b : b + 2].reshape(count * 2 * width, chans)
         part = jnp.dot(lhs, w[a, b, c], preferred_element_type=jnp.float32)
         total = part if total is None else total + part
     return total
@@ -64,6 +64,7 @@
 
     quarter = quarter_of(f)
     peers = [(f + r) % 4 for r in (2, 3, 1)]
+    order = (1 - quarter // 2, quarter // 2)
     fine_d, fine_h = 2 * d + quarter // 2, 2 * h + f % 2
     def neighbour(sd, sh):
         nd, nh = fine_d + sd, fine_h + sh
@@ -97,7 +98,10 @@
     near_edge, near_halo = 2 - core, 3 - 3 * core
     far_edge, far_halo = 1 + core, 3 * core
     has_far = (fine_h + outward >= 0) & (fine_h + outward < 2 * heights)
-    has_depth = (fine_d > 0, fine_d < 2 * depths - 1)
+
+    def has_depth(i):
+        nd = fine_d + 2 * i - 1
+        return (nd >= 0) & (nd < 2 * depths)
 
     for ref in (xh, hh):
         @pl.when(jnp.logical_not(has_far))
@@ -106,7 +110,7 @@
                 ref[row, far_halo] = jnp.zeros_like(ref[row, far_halo])
 
         for i in range(2):
-            @pl.when(jnp.logical_not(has_depth[i]))
+            @pl.when(jnp.logical_not(has_depth(i)))
             def _():
                 ref[3 * i] = jnp.zeros_like(ref[3 * i])
 
@@ -114,45 +118,43 @@
     wide = 3 - jnp.where(fine_h == 0, 1, 0) - jnp.where(fine_h == 2 * heights - 1, 1, 0)
     pl.semaphore_wait(barrier, tall * wide - 1)
 
-    def gather(g):
+    def gather(g, p):
+        q = quarter_of(g)
+        row = q // 2 if p else 1 - q // 2
         return pltpu.make_async_remote_copy(
-            src_ref=xs.at[quarter_of(g)], dst_ref=ra.at[f], send_sem=sa.at[g], recv_sem=qa.at[f],
+            src_ref=xs.at[q, row], dst_ref=ra.at[f, row], send_sem=sa.at[g, p], recv_sem=qa.at[f, p],
             device_id={"filt": g}, device_id_type=MESH)
 
-    def gathered(g):
+    def gathered(g, p):
         return pltpu.make_async_remote_copy(
-            src_ref=xs.at[quarter], dst_ref=ra.at[g], send_sem=sa.at[g], recv_sem=qa.at[g],
+            src_ref=xs.at[quarter, order[p]], dst_ref=ra.at[g, order[p]], send_sem=sa.at[g, p], recv_sem=qa.at[g, p],
             device_id={"filt": g}, device_id_type=MESH)
 
-    for g in peers:
-        gather(g).start()
+    for p in range(2):
+        for g in peers:
+            gather(g, p).start()
     ra[f] = xs[quarter]
-    for g in reversed(peers):
-        gathered(g).wait_recv()
-    for i in range(2):
-        for j in range(2):
-            xh[1 + i, 1 + j] = jnp.concatenate(
-                [ra[g, i, :, j * shard : (j + 1) * shard] for g in range(4)], axis=-1)
-
-    def halo(ref, send, recv, m):
-        i = m % 2
-        if m in NEAR:
+
+    def halo(ref, send, recv, kind, i):
+        m = 2 * kind + i
+        across = 2 * kind + 1 - i
+        if kind == NEAR:
             valid, to, step = None, m, (0, -outward)
             edge, there, here = (1 + i, near_edge), (1 + i, 3 * core), (1 + i, near_halo)
-        elif m in FAR:
+        elif kind == FAR:
             valid, to, step = has_far, m, (0, outward)
             edge, there, here = (1 + i, far_edge), (1 + i, 3 - 3 * core), (1 + i, far_halo)
-        elif m in FACE:
-            valid, to, step = has_depth[i], FACE[1 - i], (2 * i - 1, 0)
+        elif kind == FACE:
+            valid, to, step = has_depth(i), across, (2 * i - 1, 0)
             edge, there, here = (1 + i, near_edge), (3 - 3 * i, near_edge), (3 * i, near_edge)
-        elif m in REST:
-            valid, to, step = has_depth[i], REST[1 - i], (2 * i - 1, 0)
+        elif kind == REST:
+            valid, to, step = has_depth(i), across, (2 * i - 1, 0)
             edge, there, here = (1 + i, far_edge), (3 - 3 * i, far_edge), (3 * i, far_edge)
-        elif m in CORNER:
-            valid, to, step = has_depth[i] & has_far, CORNER[1 - i], (2 * i - 1, outward)
+        elif kind == CORNER:
+            valid, to, step = has_depth(i) & has_far, across, (2 * i - 1, outward)
             edge, there, here = (1 + i, far_edge), (3 - 3 * i, 3 - 3 * core), (3 * i, far_halo)
         else:
-            valid, to, step = has_depth[i], m, (0, -outward)
+            valid, to, step = has_depth(i), m, (0, -outward)
             edge, there, here = (3 * i, near_edge), (3 * i, 3 * core), (3 * i, near_halo)
         _, device = neighbour(*step)
 
@@ -176,43 +178,52 @@
         else:
             pl.when(valid)(act)
 
-    def start(refs, *messages):
-        for m in messages:
-            valid, copy, _ = halo(*refs, m)
+    def start(refs, i, *kinds):
+        for kind in kinds:
+            valid, copy, _ = halo(*refs, kind, i)
             when(valid, lambda: copy().start())
 
-    def finish(refs, *messages):
-        for m in messages:
-            valid, _, arrival = halo(*refs, m)
+    def finish(refs, i, *kinds):
+        for kind in kinds:
+            valid, _, arrival = halo(*refs, kind, i)
             when(valid, lambda: arrival().wait_recv())
 
     def forward(refs, i):
-        valid, _, arrival = halo(*refs, FACE[i])
-        _, copy, _ = halo(*refs, FORWARD[i])
+        valid, _, arrival = halo(*refs, FACE, i)
+        _, copy, _ = halo(*refs, FORWARD, i)
 
         @pl.when(valid)
         def _():
             arrival().wait_recv()
             copy().start()
 
+    sends = (FACE, FAR, CORNER, REST, NEAR)
     first, second = (xh, sb, qb), (hh, sc, qc)
-    start(first, *FACE, *FAR, *CORNER, *REST, *NEAR)
+    for p, row in enumerate(order):
+        for g in reversed(peers):
+            gathered(g, p).wait_recv()
+        for j in range(2):
+            xh[1 + row, 1 + j] = jnp.concatenate(
+                [ra[g, row, :, j * shard : (j + 1) * shard] for g in range(4)], axis=-1)
+        start(first, row, *sends)
     loads[1].wait()
     loads[3].wait()
-    forward(first, 0)
-    forward(first, 1)
-    finish(first, *NEAR, *FAR)
+    for row in order:
+        forward(first, row)
+    for row in order:
+        finish(first, row, NEAR, FAR)
     inner_taps(xh, w1, acc)
-    for row in range(2):
-        finish(first, FORWARD[row], CORNER[row], REST[row])
+    for row in order:
+        finish(first, row, FORWARD, CORNER, REST)
         hh[1 + row, 1:3] = outer_taps(xh, w1, acc, bb1, row).reshape(2, width, 4 * shard)
-        start(second, FACE[row], FAR[row], CORNER[row], REST[row], NEAR[row])
+        start(second, row, *sends)
 
     loads[2].wait()
     loads[4].wait()
-    forward(second, 0)
-    forward(second, 1)
-    finish(second, *NEAR, *FAR)
+    for row in order:
+        forward(second, row)
+    for row in order:
+        finish(second, row, NEAR, FAR)
     inner_taps(hh, w2, acc)
 
     def scatter(g, row):
@@ -228,8 +239,8 @@
             send_sem=se.at[g, row], recv_sem=qe.at[q, row],
             device_id={"filt": g}, device_id_type=MESH)
 
-    for row in range(2):
-        finish(second, FORWARD[row], CORNER[row], REST[row])
+    for row in order:
+        finish(second, row, FORWARD, CORNER, REST)
         result = outer_taps(hh, w2, acc, bb2, row)
         for g in range(4):
             part = result[:, g * shard : (g + 1) * shard]
@@ -239,11 +250,13 @@
         ro[quarter, row] = os[f, row]
 
     for g in peers:
-        gather(g).wait_send()
+        for p in range(2):
+            gather(g, p).wait_send()
     for refs in (first, second):
-        for m in range(12):
-            valid, copy, _ = halo(*refs, m)
-            when(valid, lambda: copy().wait_send())
+        for kind in range(6):
+            for i in range(2):
+                valid, copy, _ = halo(*refs, kind, i)
+                when(valid, lambda: copy().wait_send())
 
     for row in range(2):
         for g in reversed(peers):
@@ -281,7 +294,7 @@
             packed,
             packed,
             pltpu.VMEM((3, 2, 2 * width, chans), jnp.float32),
-            dma((5,)), dma((4,)), dma((4,)), dma((12,)), dma((12,)), dma((12,)), dma((12,)), dma((4, 2)), dma((4, 2)),
+            dma((5,)), dma((4, 2)), dma((4, 2)), dma((12,)), dma((12,)), dma((12,)), dma((12,)), dma((4, 2)), dma((4, 2)),
         ],
         compiler_params=pltpu.CompilerParams(
             collective_id=0, has_side_effects=True, vmem_limit_bytes=VMEM_LIMIT),

time: 28.9 us -> 29.5 us (1.021)
  Pallas kernels: 28.1 us -> 28.7 us
    pallas_call x1, Pallas kernels: 28.1 us -> 28.7 us  [body(): pl.pallas_call(functools.partial(kernel, depths, heights), out_shape=jax....]
where the time goes in v6:
time: 29.5 us; the launch traced here: 29.4 us
  Pallas kernels  28.7 us (97%)
  local copies, waits for them, and re-layouts  0.71 us (2%)
    pallas_call x1, Pallas kernels, body(): pl.pallas_call(functools.partial(kernel, depths, heights), out_shape=jax....  28.7 us
    unnamed x1, local copies, waits for them, and re-layouts  0.71 us

profile of v6, /device:TPU:1, one launch (start us, length us, event | category | flops | bytes accessed | tf_op | source)
XLA Modules:
  0.0 29.4 jit_solution(17820967141339547152)
XLA Ops:
  0.0 28.7 %shard_map.55 = bf16[4,4,64,64]{3,2,1,0:T(8,128)(2,1)S(1)} custom-call(bf16[4,4,64,64]{3,2,1,0:T(8,128)(2,1)} %vol.1, bf16[3,3,3,256,256]{4,3,2,1,0:T(8,128)(2,1)} %k1.1, f32[1,256]{1,0:T(1,128)} %bitcast.2, bf16[3,3,3,256,256]{4,3,2,1,0:T(8,128)(2,1)} %k2.1, f32[1,256]{1,0:T(1,128)} %bitcast.3), custom_call_target="tpu_custom_call" | custom-call | tf_op jit(solution)/shard_map/pallas_call | solution.py:279
  28.7 0.7 %copy.7 = bf16[4,4,64,64]{3,2,1,0:T(8,128)(2,1)} copy(bf16[4,4,64,64]{3,2,1,0:T(8,128)(2,1)S(1)} %shard_map.55) | data formatting | bytes 262144

commit v7 on v4

--- a/solution.py
+++ b/solution.py
@@ -199,22 +199,6 @@
     start(first, *FACE, *FAR, *CORNER, *REST, *NEAR)
     loads[1].wait()
     loads[3].wait()
-    forward(first, 0)
-    forward(first, 1)
-    finish(first, *NEAR, *FAR)
-    inner_taps(xh, w1, acc)
-    for row in range(2):
-        finish(first, FORWARD[row], CORNER[row], REST[row])
-        hh[1 + row, 1:3] = outer_taps(xh, w1, acc, bb1, row).reshape(2, width, 4 * shard)
-        start(second, FACE[row], FAR[row], CORNER[row], REST[row], NEAR[row])
-
-    loads[2].wait()
-    loads[4].wait()
-    forward(second, 0)
-    forward(second, 1)
-    finish(second, *NEAR, *FAR)
-    inner_taps(hh, w2, acc)
-
     def scatter(g, row):
         return pltpu.make_async_remote_copy(
             src_ref=os.at[g, row], dst_ref=ro.at[quarter, row],
@@ -228,15 +212,40 @@
             send_sem=se.at[g, row], recv_sem=qe.at[q, row],
             device_id={"filt": g}, device_id_type=MESH)
 
-    for row in range(2):
-        finish(second, FORWARD[row], CORNER[row], REST[row])
-        result = outer_taps(hh, w2, acc, bb2, row)
-        for g in range(4):
-            part = result[:, g * shard : (g + 1) * shard]
-            os[g, row] = jnp.concatenate([part[:width], part[width:]], axis=-1)
-        for g in peers:
-            scatter(g, row).start()
-        ro[quarter, row] = os[f, row]
+    def both(order):
+        for row in order:
+            forward(first, row)
+        finish(first, *NEAR, *FAR)
+        inner_taps(xh, w1, acc)
+        for row in order:
+            finish(first, FORWARD[row], CORNER[row], REST[row])
+            hh[1 + row, 1:3] = outer_taps(xh, w1, acc, bb1, row).reshape(2, width, 4 * shard)
+            start(second, FACE[row], FAR[row], CORNER[row], REST[row], NEAR[row])
+
+        loads[2].wait()
+        loads[4].wait()
+        for row in order:
+            forward(second, row)
+        finish(second, *NEAR, *FAR)
+        inner_taps(hh, w2, acc)
+
+        for row in order:
+            finish(second, FORWARD[row], CORNER[row], REST[row])
+            result = outer_taps(hh, w2, acc, bb2, row)
+            for g in range(4):
+                part = result[:, g * shard : (g + 1) * shard]
+                os[g, row] = jnp.concatenate([part[:width], part[width:]], axis=-1)
+            for g in peers:
+                scatter(g, row).start()
+            ro[quarter, row] = os[f, row]
+
+    @pl.when(quarter // 2 == 0)
+    def _():
+        both((1, 0))
+
+    @pl.when(quarter // 2 == 1)
+    def _():
+        both((0, 1))
 
     for g in peers:
         gather(g).wait_send()

time: 28.9 us -> 29.2 us (1.010)
  Pallas kernels: 28.1 us -> 28.4 us
where the time goes in v7:
time: 29.2 us; the launch traced here: 29.1 us
  Pallas kernels  28.4 us (97%)
  local copies, waits for them, and re-layouts  0.71 us (2%)
    pallas_call x1, Pallas kernels, body(): pl.pallas_call(functools.partial(kernel, depths, heights), out_shape=jax....  28.4 us
    unnamed x1, local copies, waits for them, and re-layouts  0.71 us

profile of v7, /device:TPU:1, one launch (start us, length us, event | category | flops | bytes accessed | tf_op | source)
XLA Modules:
  0.0 29.1 jit_solution(491281273942281915)
XLA Ops:
  0.0 28.4 %shard_map.55 = bf16[4,4,64,64]{3,2,1,0:T(8,128)(2,1)S(1)} custom-call(bf16[4,4,64,64]{3,2,1,0:T(8,128)(2,1)} %vol.1, bf16[3,3,3,256,256]{4,3,2,1,0:T(8,128)(2,1)} %k1.1, f32[1,256]{1,0:T(1,128)} %bitcast.2, bf16[3,3,3,256,256]{4,3,2,1,0:T(8,128)(2,1)} %k2.1, f32[1,256]{1,0:T(1,128)} %bitcast.3), custom_call_target="tpu_custom_call" | custom-call | tf_op jit(solution)/shard_map/pallas_call | solution.py:275
  28.4 0.7 %copy.7 = bf16[4,4,64,64]{3,2,1,0:T(8,128)(2,1)} copy(bf16[4,4,64,64]{3,2,1,0:T(8,128)(2,1)S(1)} %shard_map.55) | data formatting | bytes 262144

commit v8 on v4

--- a/solution.py
+++ b/solution.py
@@ -10,7 +10,7 @@
 MESH = pl.DeviceIdType.MESH
 VMEM_LIMIT = 40_000_000
 STEPS = tuple((a, b) for a in (-1, 0, 1) for b in (-1, 0, 1) if (a, b) != (0, 0))
-NEAR, FAR, FACE, REST, CORNER, FORWARD = (range(2 * i, 2 * i + 2) for i in range(6))
+NEAR, FAR, FACE, REST, CORNER, INNER = (range(2 * i, 2 * i + 2) for i in range(6))
 
 
 def flip_of(d):
@@ -152,8 +152,8 @@
             valid, to, step = has_depth[i] & has_far, CORNER[1 - i], (2 * i - 1, outward)
             edge, there, here = (1 + i, far_edge), (3 - 3 * i, 3 - 3 * core), (3 * i, far_halo)
         else:
-            valid, to, step = has_depth[i], m, (0, -outward)
-            edge, there, here = (3 * i, near_edge), (3 * i, 3 * core), (3 * i, near_halo)
+            valid, to, step = has_depth[i], INNER[1 - i], (2 * i - 1, -outward)
+            edge, there, here = (1 + i, near_edge), (3 - 3 * i, 3 * core), (3 * i, near_halo)
         _, device = neighbour(*step)
 
         def copy():
@@ -186,32 +186,19 @@
             valid, _, arrival = halo(*refs, m)
             when(valid, lambda: arrival().wait_recv())
 
-    def forward(refs, i):
-        valid, _, arrival = halo(*refs, FACE[i])
-        _, copy, _ = halo(*refs, FORWARD[i])
-
-        @pl.when(valid)
-        def _():
-            arrival().wait_recv()
-            copy().start()
-
     first, second = (xh, sb, qb), (hh, sc, qc)
-    start(first, *FACE, *FAR, *CORNER, *REST, *NEAR)
+    start(first, *CORNER, *FAR, *INNER, *FACE, *REST, *NEAR)
     loads[1].wait()
     loads[3].wait()
-    forward(first, 0)
-    forward(first, 1)
     finish(first, *NEAR, *FAR)
     inner_taps(xh, w1, acc)
     for row in range(2):
-        finish(first, FORWARD[row], CORNER[row], REST[row])
+        finish(first, CORNER[row], INNER[row], FACE[row], REST[row])
         hh[1 + row, 1:3] = outer_taps(xh, w1, acc, bb1, row).reshape(2, width, 4 * shard)
-        start(second, FACE[row], FAR[row], CORNER[row], REST[row], NEAR[row])
+        start(second, CORNER[row], FAR[row], INNER[row], FACE[row], REST[row], NEAR[row])
 
     loads[2].wait()
     loads[4].wait()
-    forward(second, 0)
-    forward(second, 1)
     finish(second, *NEAR, *FAR)
     inner_taps(hh, w2, acc)
 
@@ -229,7 +216,7 @@
             device_id={"filt": g}, device_id_type=MESH)
 
     for row in range(2):
-        finish(second, FORWARD[row], CORNER[row], REST[row])
+        finish(second, CORNER[row], INNER[row], FACE[row], REST[row])
         result = outer_taps(hh, w2, acc, bb2, row)
         for g in range(4):
             part = result[:, g * shard : (g + 1) * shard]

time: 28.9 us -> 29 us (level)
  no operation moved by 1% of the time
where the time goes in v8:
time: 29 us; the launch traced here: 28.9 us
  Pallas kernels  28.1 us (97%)
  local copies, waits for them, and re-layouts  0.71 us (2%)
    pallas_call x1, Pallas kernels, body(): pl.pallas_call(functools.partial(kernel, depths, heights), out_shape=jax....  28.1 us
    unnamed x1, local copies, waits for them, and re-layouts  0.71 us

profile of v8, /device:TPU:1, one launch (start us, length us, event | category | flops | bytes accessed | tf_op | source)
XLA Modules:
  0.0 28.9 jit_solution(4451950072079143139)
XLA Ops:
  0.0 28.1 %shard_map.55 = bf16[4,4,64,64]{3,2,1,0:T(8,128)(2,1)S(1)} custom-call(bf16[4,4,64,64]{3,2,1,0:T(8,128)(2,1)} %vol.1, bf16[3,3,3,256,256]{4,3,2,1,0:T(8,128)(2,1)} %k1.1, f32[1,256]{1,0:T(1,128)} %bitcast.2, bf16[3,3,3,256,256]{4,3,2,1,0:T(8,128)(2,1)} %k2.1, f32[1,256]{1,0:T(1,128)} %bitcast.3), custom_call_target="tpu_custom_call" | custom-call | tf_op jit(solution)/shard_map/pallas_call | solution.py:253
  28.2 0.7 %copy.7 = bf16[4,4,64,64]{3,2,1,0:T(8,128)(2,1)} copy(bf16[4,4,64,64]{3,2,1,0:T(8,128)(2,1)S(1)} %shard_map.55) | data formatting | bytes 262144

commit v9 on v4

--- a/solution.py
+++ b/solution.py
@@ -196,7 +196,7 @@
             copy().start()
 
     first, second = (xh, sb, qb), (hh, sc, qc)
-    start(first, *FACE, *FAR, *CORNER, *REST, *NEAR)
+    start(first, *FACE, *CORNER, *REST, *FAR, *NEAR)
     loads[1].wait()
     loads[3].wait()
     forward(first, 0)
@@ -206,7 +206,7 @@
     for row in range(2):
         finish(first, FORWARD[row], CORNER[row], REST[row])
         hh[1 + row, 1:3] = outer_taps(xh, w1, acc, bb1, row).reshape(2, width, 4 * shard)
-        start(second, FACE[row], FAR[row], CORNER[row], REST[row], NEAR[row])
+        start(second, FACE[row], CORNER[row], REST[row], FAR[row], NEAR[row])
 
     loads[2].wait()
     loads[4].wait()

time: 28.9 us -> 29.5 us (1.021)
  Pallas kernels: 28.1 us -> 28.7 us
    pallas_call x1, Pallas kernels: 28.1 us -> 28.7 us  [body(): pl.pallas_call(functools.partial(kernel, depths, heights), out_shape=jax....]
where the time goes in v9:
time: 29.5 us; the launch traced here: 29.4 us
  Pallas kernels  28.7 us (97%)
  local copies, waits for them, and re-layouts  0.71 us (2%)
    pallas_call x1, Pallas kernels, body(): pl.pallas_call(functools.partial(kernel, depths, heights), out_shape=jax....  28.7 us
    unnamed x1, local copies, waits for them, and re-layouts  0.71 us

profile of v9, /device:TPU:1, one launch (start us, length us, event | category | flops | bytes accessed | tf_op | source)
XLA Modules:
  0.0 29.4 jit_solution(17582242142457134033)
XLA Ops:
  0.0 28.7 %shard_map.55 = bf16[4,4,64,64]{3,2,1,0:T(8,128)(2,1)S(1)} custom-call(bf16[4,4,64,64]{3,2,1,0:T(8,128)(2,1)} %vol.1, bf16[3,3,3,256,256]{4,3,2,1,0:T(8,128)(2,1)} %k1.1, f32[1,256]{1,0:T(1,128)} %bitcast.2, bf16[3,3,3,256,256]{4,3,2,1,0:T(8,128)(2,1)} %k2.1, f32[1,256]{1,0:T(1,128)} %bitcast.3), custom_call_target="tpu_custom_call" | custom-call | tf_op jit(solution)/shard_map/pallas_call | solution.py:266
  28.7 0.7 %copy.7 = bf16[4,4,64,64]{3,2,1,0:T(8,128)(2,1)} copy(bf16[4,4,64,64]{3,2,1,0:T(8,128)(2,1)S(1)} %shard_map.55) | data formatting | bytes 262144
